TPU v7x, 256 devices: a whole 4x4x8 slice. The times are simulated.
256 devices in a mesh: seq: 16 (over x, z_hi), mp: 16 (over y, z_lo, core).
Axes of the slice: x: 4, y: 4, z: 8 (z_hi: 4, z_lo: 2; z = z_hi * 2 + z_lo), core: 2. Of those that a mesh axis runs over, the one named last changes fastest.
Arguments:
- hidden: bfloat16 [4096, 4096], P('seq', 'mp'), may hold values from -6 to 6
- cotangent: bfloat16 [4096, 4096], P('seq', 'mp'), may hold values from -6 to 6
- neighbour_ids: int32 [64, 2, 128], P('seq'), may hold values from 0 to 63999
- neighbour_lengths: int32 [64, 2], replicated, may hold values from 1 to 128
- embed_table: bfloat16 [64000, 896], P('mp'), may hold values from -6 to 6
- enc_up: bfloat16 [3584, 896], P('mp'), may hold values from -0.1875 to 0.1875
- enc_down: bfloat16 [3584, 896], P('mp'), may hold values from -0.09375 to 0.09375
- w_query: bfloat16 [4096, 32, 128], P('seq', 'mp'), may hold values from -0.125 to 0.125
- w_keyval: bfloat16 [896, 32, 2, 128], P('seq', 'mp'), may hold values from -0.1875 to 0.1875
- w_out: bfloat16 [4096, 32, 128], P('seq', 'mp'), may hold values from -0.75 to 0.75
Outputs:
- cca_out: bfloat16 [4096, 4096], P('seq', 'mp')
- hidden_grad: bfloat16 [4096, 4096], P('seq', 'mp')
All inputs are finite; a program needn't handle non-finite values.
Results may differ from a plain program's by a relative error of at most 0.012.
Values may be sent and summed in bfloat16 or wider, within the bound.
A program may use at most 128 MiB of HBM per device.

v0:
```python
import jax
import jax.numpy as jnp
from jax import lax
from jax.sharding import PartitionSpec as P


def from_behind(shard, axis, by):
    count = lax.axis_size(axis)
    pairs = [(i, i + by) for i in range(count) if 0 <= i + by < count]
    return lax.ppermute(shard, axis, pairs)


def rms_rows(values):
    return values * lax.rsqrt(jnp.mean(values * values, axis=-1, keepdims=True) + 1e-06)


def shift_rows(flat, span_len):
    width = flat.shape[1]
    front = jnp.zeros((1, width), flat.dtype)
    back = jnp.zeros((span_len - 1, width), flat.dtype)
    return jnp.concatenate([front, flat, back], axis=0)


def contract_heads(left, right):
    return lax.dot_general(
        left, right, (((1,), (1,)), ((), ())), preferred_element_type=jnp.float32
    )


def per_device(
    hidden,
    cotangent,
    neighbour_ids,
    neighbour_lengths,
    embed_table,
    enc_up,
    enc_down,
    w_query,
    w_keyval,
    w_out,
):
    spans_here, neigh, nlen = neighbour_ids.shape
    tok_rows = hidden.shape[0]
    span_len = tok_rows // spans_here
    groups = spans_here + 1
    keys_per = neigh * nlen
    id_rows = spans_here * keys_per
    vocab_here = embed_table.shape[0]
    local_ids = neighbour_ids.reshape(id_rows) - lax.axis_index("mp") * vocab_here
    inside = jnp.logical_and(local_ids >= 0, local_ids < vocab_here)
    picked = jnp.take(embed_table, jnp.clip(local_ids, 0, vocab_here - 1), axis=0)
    masked = jnp.where(inside[:, None], picked, jnp.zeros((), picked.dtype))
    emb_share = (
        lax.psum_scatter(masked, "mp", scatter_dimension=0, tiled=True)
        .astype(jnp.float32)
        .astype(jnp.bfloat16)
    )
    emb = lax.all_gather(emb_share, "mp", axis=0, tiled=True)
    whole_hidden, whole_cot = (
        lax.all_gather(hidden, "mp", axis=1, tiled=True),
        lax.all_gather(cotangent, "mp", axis=1, tiled=True),
    )
    wq_full, wkv_full, wo_full = (
        lax.all_gather(w_query, "seq", axis=0, tiled=True),
        lax.all_gather(w_keyval, "seq", axis=0, tiled=True),
        lax.all_gather(w_out, "seq", axis=0, tiled=True),
    )
    width = whole_hidden.shape[1]
    heads_here = wq_full.shape[1]
    head_dim = wq_full.shape[2]
    inner = heads_here * head_dim
    scale = head_dim ** (-0.5)
    wq_flat = wq_full.reshape(width, inner)
    wo_flat = wo_full.reshape(width, inner)
    enc_width = emb.shape[1]
    wkv_flat = wkv_full.reshape(enc_width, 2 * inner)
    emb_wide = emb.astype(jnp.float32)
    normed = rms_rows(emb_wide).astype(jnp.bfloat16)
    act_cols = jax.nn.gelu(contract_heads(enc_up, normed)).astype(jnp.bfloat16)
    ffn_part = lax.dot_general(
        act_cols, enc_down, (((0,), (0,)), ((), ())), preferred_element_type=jnp.float32
    )
    total = lax.psum(ffn_part, "mp")
    encoded = rms_rows(emb_wide + total).astype(jnp.bfloat16)
    keyval = jnp.dot(encoded, wkv_flat, preferred_element_type=jnp.float32).astype(jnp.bfloat16)
    keyval = keyval.reshape(spans_here, keys_per, 2 * inner)
    last_rows = encoded.reshape(spans_here, keys_per, enc_width)[spans_here - 1]
    prev_rows = from_behind(last_rows, "seq", 1)
    previous = jnp.dot(prev_rows, wkv_flat, preferred_element_type=jnp.float32).astype(jnp.bfloat16)
    keyval_all = jnp.concatenate([previous[None], keyval], axis=0).reshape(
        groups, keys_per, heads_here, 2, head_dim
    )
    keys = keyval_all[:, :, :, 0]
    values = keyval_all[:, :, :, 1]
    position = lax.axis_index("seq")
    lens_pad = jnp.concatenate([jnp.ones((1, neigh), jnp.int32), neighbour_lengths], axis=0)
    lens = lax.dynamic_slice_in_dim(lens_pad, position * spans_here, groups, 0)
    key_mask = (jnp.arange(nlen, dtype=jnp.int32)[None, None, :] < lens[:, :, None]).reshape(
        groups, keys_per
    )
    valid = jnp.logical_or(jnp.arange(groups) > 0, position > 0).astype(jnp.float32)
    query = jnp.dot(whole_hidden, wq_flat, preferred_element_type=jnp.float32).astype(jnp.bfloat16)
    query_g = shift_rows(query, span_len).reshape(groups, span_len, heads_here, head_dim)
    scores = (
        jnp.einsum("gqhd,gkhd->ghqk", query_g, keys, preferred_element_type=jnp.float32) * scale
    )
    expo = jnp.where(key_mask[:, None, None, :], jnp.exp(scores), 0.0)
    prob = expo / jnp.sum(expo, axis=-1, keepdims=True) * valid[:, None, None, None]
    prob_low = prob.astype(jnp.bfloat16)
    attn = jnp.einsum(
        "ghqk,gkhd->gqhd", prob_low, values, preferred_element_type=jnp.float32
    ).astype(jnp.bfloat16)
    attn_flat = attn.reshape(groups * span_len, inner)[1 : tok_rows + 1]
    out_part = contract_heads(attn_flat, wo_flat)
    d_attn = jnp.dot(whole_cot, wo_flat, preferred_element_type=jnp.float32).astype(jnp.bfloat16)
    d_group = shift_rows(d_attn, span_len).reshape(groups, span_len, heads_here, head_dim)
    d_prob = jnp.einsum("gqhd,gkhd->ghqk", d_group, values, preferred_element_type=jnp.float32)
    delta = jnp.sum(prob * d_prob, axis=-1, keepdims=True)
    d_score = (prob * (d_prob - delta) * scale).astype(jnp.bfloat16)
    d_query = jnp.einsum(
        "ghqk,gkhd->gqhd", d_score, keys, preferred_element_type=jnp.float32
    ).astype(jnp.bfloat16)
    d_flat = d_query.reshape(groups * span_len, inner)[1 : tok_rows + 1]
    grad_part = contract_heads(d_flat, wq_flat)
    out_sum, grad_sum = (
        lax.psum_scatter(out_part, "mp", scatter_dimension=1, tiled=True),
        lax.psum_scatter(grad_part, "mp", scatter_dimension=1, tiled=True),
    )
    cca_out = out_sum.astype(jnp.bfloat16)
    hidden_grad = grad_sum.astype(jnp.bfloat16)
    return (cca_out, hidden_grad)


def solution(mesh):
    return jax.shard_map(
        per_device,
        mesh=mesh,
        in_specs=(
            P("seq", "mp"),
            P("seq", "mp"),
            P("seq", None, None),
            P(),
            P("mp", None),
            P("mp", None),
            P("mp", None),
            P("seq", "mp", None),
            P("seq", "mp", None, None),
            P("seq", "mp", None),
        ),
        out_specs=(P("seq", "mp"), P("seq", "mp")),
        check_vma=False,
    )
```

profile of v0, /device:TPU:1, one launch (start us, length us, event | category | flops | bytes accessed | tf_op | source)
XLA Modules:
  0.0 664.8 jit_solution(14386013505363016932)
XLA Ops:
  7.2 0.0 reduce-scatter.4.cloned.1.call-start
  7.2 0.7 subtract_clamp_fusion
  8.0 0.7 compare_and_fusion
  8.7 8.6 %gather_fusion = bf16[1024,896]{1,0:T(8,128)(2,1)S(1)} fusion(bf16[4000,896]{1,0:T(8,128)(2,1)} %param.14, s32[1024]{0:T(1024)S(1)} %broadcast_clamp_fusion), kind=kCustom, calls=%fused_computation | custom fusion | bytes 3674112 | tf_op jit(solution)/shard_map/jit(_take)/gather | solution.py:51
  17.3 1.9 select_select_fusion
  19.2 0.0 all-gather.6.cloned.1.call-start
  19.3 67.7 %reduce-scatter.4.cloned.1.call-done = bf16[64,896]{1,0:T(8,128)(2,1)} async-done(((bf16[1024,896]{1,0:T(8,128)(2,1)}), bf16[64,896]{1,0:T(8,128)(2,1)}) %reduce-scatter.4.cloned.1.call-update) | async-done | bytes 114704 | tf_op jit(solution)/shard_map/reduce_scatter | solution.py:54
  87.0 0.0 all-gather.10.cloned.1.call-start
  87.0 0.7 all-gather.10.cloned.1.call-update
  87.7 0.0 all-gather.8.cloned.1.call-start
  87.7 0.5 all-gather.8.cloned.1.call-update
  88.3 0.0 all-gather.12.cloned.1.call-start
  88.3 0.5 all-gather.12.cloned.1.call-update
  88.9 0.5 all-gather.14.cloned.1.call-update
  89.4 0.0 all-reduce.3.cloned.1.call-start
  89.5 36.3 %all-gather.6.cloned.1.call-done = bf16[1024,896]{1,0:T(8,128)(2,1)} async-done(((bf16[64,896]{1,0:T(8,128)(2,1)}), bf16[1024,896]{1,0:T(8,128)(2,1)}) %all-gather.6.cloned.1.call-update) | async-done | bytes 1835024 | tf_op jit(solution)/shard_map/all_gather | solution.py:58
  125.8 1.9 fusion.1
  127.8 4.9 fusion.50
  132.7 0.0 reduce-scatter.8.cloned.1.call-start
  132.8 0.7 copy-done.9
  133.5 58.7 %all_gather.19 = bf16[896,2,2,128]{3,2,1,0:T(2,128)(2,1)S(1)} all-gather(bf16[56,2,2,128]{3,2,1,0:T(2,128)(2,1)S(1)} %copy-done.9), channel_id=1, replica_groups=mesh['seq'=16,'mp'=16] {'seq'}, dimensions={0}, use_global_device_ids=true | all-gather | bytes 974848 | tf_op jit(solution)/shard_map/all_gather | solution.py:65
  192.3 0.3 reshape.123
  192.6 0.1 pad_dynamic-slice_fusion
  192.7 0.1 copy.26
  192.8 0.1 pad.6.clone
  192.9 0.1 broadcast_bitcast_fusion
  193.0 0.3 all-gather.10.cloned.1.call-done
  193.3 39.1 %all-gather.8.cloned.1.call-done = bf16[256,4096]{1,0:T(8,128)(2,1)} async-done(((bf16[256,256]{1,0:T(8,128)(2,1)}), bf16[256,4096]{1,0:T(8,128)(2,1)}) %all-gather.8.cloned.1.call-update) | async-done | bytes 2097168 | tf_op jit(solution)/shard_map/all_gather | solution.py:60
  232.3 2.9 fusion.29
  235.3 57.2 %all-gather.12.cloned.1.call-done = bf16[4096,2,128]{2,1,0:T(2,128)(2,1)} async-done(((bf16[256,2,128]{2,1,0:T(2,128)(2,1)}), bf16[4096,2,128]{2,1,0:T(2,128)(2,1)}) %all-gather.12.cloned.1.call-update) | async-done | bytes 2097168 | tf_op jit(solution)/shard_map/all_gather | solution.py:66
  292.5 40.8 %all-gather.14.cloned.1.call-done = bf16[256,4096]{1,0:T(8,128)(2,1)} async-done(((bf16[256,256]{1,0:T(8,128)(2,1)}), bf16[256,4096]{1,0:T(8,128)(2,1)}) %all-gather.14.cloned.1.call-update) | async-done | bytes 2097168 | tf_op jit(solution)/shard_map/all_gather | solution.py:61
  333.3 3.1 fusion.32
  336.4 135.9 %all-reduce.3.cloned.1.call-done = f32[1024,896]{1,0:T(8,128)} async-done(((f32[1024,896]{1,0:T(8,128)}), f32[1024,896]{1,0:T(8,128)}) %all-reduce.3.cloned.1.call-update) | async-done | bytes 3670032 | tf_op jit(solution)/shard_map/psum | solution.py:83
  472.3 2.8 multiply_reduce_fusion
  475.1 0.3 copy-done.2
  475.5 0.5 multiply_convert_fusion
  475.9 1.3 copy-done.3
  477.2 0.8 slice.23
  478.0 4.9 collective-permute-start
  482.9 0.2 maximum_maximum_fusion.1
  483.1 0.7 reshape.125
  483.8 0.7 reshape.128
  484.5 2.7 convolution_convert_fusion
  487.3 0.3 concatenate.18
  487.6 14.1 %collective-permute-done = bf16[256,896]{1,0:T(8,128)(2,1)} collective-permute-done((bf16[256,896]{1,0:T(8,128)(2,1)}, bf16[256,896]{1,0:T(8,128)(2,1)}, u32[]{:S(2)}, u32[]{:S(2)}) %collective-permute-start) | collective-permute-done | bytes 458784 | tf_op jit(solution)/shard_map/ppermute | solution.py:10
  501.6 1.4 convolution_convert_fusion.1
  503.1 0.1 concatenate.17
  503.2 0.3 copy_dynamic-update-slice_fusion
  503.6 0.3 fusion.54
  503.9 0.7 copy-done.7
  504.7 0.4 fusion.23
  505.0 0.8 copy-done.12
  505.9 1.1 divide_multiply_fusion
  506.9 1.9 fusion.36
  508.9 0.2 copy.30
  509.1 2.7 fusion.7
  511.8 0.0 reduce-scatter.6.cloned.1.call-start
  511.9 2.0 fusion.35
  513.9 0.2 copy.28
  514.1 2.7 fusion.5
  516.8 65.6 %reduce-scatter.8.cloned.1.call-done = f32[256,256]{1,0:T(8,128)} async-done(((f32[256,4096]{1,0:T(8,128)}), f32[256,256]{1,0:T(8,128)}) %reduce-scatter.8.cloned.1.call-update) | async-done | bytes 262160 | tf_op jit(solution)/shard_map/reduce_scatter | solution.py:127
  582.4 1.6 convert_element_type.73
  584.1 72.6 %reduce-scatter.6.cloned.1.call-done = f32[256,256]{1,0:T(8,128)} async-done(((f32[256,4096]{1,0:T(8,128)}), f32[256,256]{1,0:T(8,128)}) %reduce-scatter.6.cloned.1.call-update) | async-done | bytes 262160 | tf_op jit(solution)/shard_map/reduce_scatter | solution.py:126
  656.6 1.6 convert_element_type.68
  (41 shorter events, 0.3 us)
Async XLA Ops:
  7.2 120.6 %copy-start = (bf16[224,896]{1,0:T(8,128)(2,1)S(1)}, bf16[224,896]{1,0:T(8,128)(2,1)}, u32[]{:S(2)}) copy-start(bf16[224,896]{1,0:T(8,128)(2,1)} %param.16) | copy-start | bytes 1204228
  7.2 79.8 %reduce-scatter.4.cloned.1.call-start = ((), (), s32[]{:S(2)}) async-start(), calls=%async_computation.3 | async-start | bytes 1949696 | tf_op jit(solution)/shard_map/reduce_scatter | solution.py:54
  19.2 108.6 %copy-start.11 = (bf16[224,896]{1,0:T(8,128)(2,1)S(1)}, bf16[224,896]{1,0:T(8,128)(2,1)}, u32[]{:S(2)}) copy-start(bf16[224,896]{1,0:T(8,128)(2,1)} %param.15) | copy-start | bytes 1204228
  19.2 106.6 %all-gather.6.cloned.1.call-start = ((), (), s32[]{:S(2)}) async-start(), calls=%async_computation.4 | async-start | bytes 1949696 | tf_op jit(solution)/shard_map/all_gather | solution.py:58
  87.0 106.3 %all-gather.10.cloned.1.call-start = ((), (), s32[]{:S(2)}) async-start(), calls=%async_computation.7 | async-start | bytes 2228224 | tf_op jit(solution)/shard_map/all_gather | solution.py:64
  87.7 144.6 %all-gather.8.cloned.1.call-start = ((), (), s32[]{:S(2)}) async-start(), calls=%async_computation.6 | async-start | bytes 2228224 | tf_op jit(solution)/shard_map/all_gather | solution.py:60
  88.3 204.2 %all-gather.12.cloned.1.call-start = ((), (), s32[]{:S(2)}) async-start(), calls=%async_computation.8 | async-start | bytes 2228224 | tf_op jit(solution)/shard_map/all_gather | solution.py:66
  88.9 244.4 %all-gather.14.cloned.1.call-start = ((), (), s32[]{:S(2)}) async-start(), calls=%async_computation.10 | async-start | bytes 2228224 | tf_op jit(solution)/shard_map/all_gather | solution.py:61
  89.4 382.9 %all-reduce.3.cloned.1.call-start = ((), (), s32[]{:S(2)}) async-start(), calls=%async_computation.5 | async-start | bytes 7340032 | tf_op jit(solution)/shard_map/psum | solution.py:83
  132.7 0.8 copy-start.9
  132.7 59.9 %copy-start.10 = (s32[64,2]{0,1:T(2,128)S(1)}, s32[64,2]{0,1:T(2,128)}, u32[]{:S(2)}) copy-start(s32[64,2]{0,1:T(2,128)} %param.13) | copy-start | bytes 1540
  132.7 449.7 %reduce-scatter.8.cloned.1.call-start = ((), (), s32[]{:S(2)}) async-start(), calls=%async_computation.11 | async-start | bytes 4456448 | tf_op jit(solution)/shard_map/reduce_scatter | solution.py:127
  333.3 139.0 %copy-start.1 = (bf16[1024,896]{1,0:T(8,128)(2,1)S(1)}, bf16[1024,896]{1,0:T(8,128)(2,1)}, u32[]{:S(2)}) copy-start(bf16[1024,896]{1,0:T(8,128)(2,1)} %all-gather.6.cloned.1.call-done) | copy-start | bytes 5505028
  472.3 3.1 copy-start.2
  475.9 1.3 copy-start.3
  478.0 23.6 %collective-permute-start = (bf16[256,896]{1,0:T(8,128)(2,1)}, bf16[256,896]{1,0:T(8,128)(2,1)}, u32[]{:S(2)}, u32[]{:S(2)}) collective-permute-start(bf16[256,896]{1,0:T(8,128)(2,1)} %slice.23), channel_id=1, source_target_pairs={{0,16},{16,32},{32,48},{48,64},{64,80},{80,96},{96,112},{112,128},... | collective-permute-start | bytes 1376264 | tf_op jit(solution)/shard_map/ppermute | solution.py:10
  487.6 16.0 %copy-start.6 = (bf16[5,64,2,128]{3,2,1,0:T(2,128)(2,1)S(1)}, bf16[5,64,2,128]{3,2,1,0:T(2,128)(2,1)}, u32[]{:S(2)}) copy-start(bf16[5,64,2,128]{3,2,1,0:T(2,128)(2,1)} %reshape.128) | copy-start | bytes 491524
  503.2 1.5 copy-start.8
  503.6 1.1 copy-start.7
  505.0 0.8 copy-start.12
  505.9 3.2 copy-start.5
  511.8 2.3 copy-start.4
  511.8 144.8 %reduce-scatter.6.cloned.1.call-start = ((), (), s32[]{:S(2)}) async-start(), calls=%async_computation.9 | async-start | bytes 4456448 | tf_op jit(solution)/shard_map/reduce_scatter | solution.py:126
Sparse Core Ops, SparseCore 0:
  19.3 67.5 reduce-scatter.3
  88.8 36.9 all-gather.5
  128.3 64.9 all-gather.9
  194.9 37.3 all-gather.7
  234.6 57.8 all-gather.11
  294.1 39.1 all-gather.13
  336.0 136.2 all-reduce.2
  511.9 70.4 reduce-scatter.7
  585.0 71.5 reduce-scatter.5
where the time goes:
time: 667 us; the launch traced here: 665 us
  waiting for transfers between devices  532 us (80%)
  blocking collectives  58.7 us (9%)
  matrix products  25.1 us (4%)
  local copies, waits for them, and re-layouts  16.6 us (2%)
  between operations  14.2 us (2%)
  other arithmetic  13 us (2%)
    psum x1, waiting for transfers between devices, per_device(): total = lax.psum(ffn_part, 'mp')  136 us
    reduce_scatter x1, waiting for transfers between devices, per_device(): lax.psum_scatter(out_part, 'mp', scatter_dimension=1, tiled=True)  72.6 us
    reduce_scatter x1, waiting for transfers between devices, per_device(): lax.psum_scatter(masked, 'mp', scatter_dimension=0, tiled=True)  67.7 us
    reduce_scatter x1, waiting for transfers between devices, per_device(): lax.psum_scatter(grad_part, 'mp', scatter_dimension=1, tiled=True)  65.6 us
    all_gather x1, blocking collectives, per_device(): lax.all_gather(w_keyval, 'seq', axis=0, tiled=True)  58.7 us
    all_gather x1, waiting for transfers between devices, per_device(): lax.all_gather(w_out, 'seq', axis=0, tiled=True)  57.2 us
    all_gather x1, waiting for transfers between devices, per_device(): lax.all_gather(cotangent, 'mp', axis=1, tiled=True)  40.8 us
    all_gather x1, waiting for transfers between devices, per_device(): lax.all_gather(hidden, 'mp', axis=1, tiled=True)  39.1 us
  transfers between devices with their start and end apart: 10, of which 10 were waited for; matrix products, arithmetic and copies ran while one was open for 4% of the time, Pallas kernels for 0%

commit v1 on v0

v1 whole, which is shorter than its diff:
```python
import functools

import jax
import jax.numpy as jnp
from jax import lax
from jax.experimental import pallas as pl
from jax.experimental.pallas import tpu as pltpu
from jax.sharding import PartitionSpec as P

MESH = pl.DeviceIdType.MESH
F32 = jnp.float32
BF16 = jnp.bfloat16


class Place:
    def __init__(self):
        s = lax.axis_index("seq")
        m = lax.axis_index("mp")
        self.s, self.m = s, m
        self.x, self.zh = s // 4, s % 4
        self.y, self.zl, self.c = m // 4, (m // 2) % 2, m % 2
        self.sib = (s, self.mp(0, self.zl, 1 - self.c))
        self.zn = (s, self.mp(0, 1 - self.zl, self.c))
        self.yp = (s, self.mp(1, self.zl, self.c))
        self.ym = (s, self.mp(3, self.zl, self.c))
        self.zp = (self.seq(0, 1), m)
        self.zm = (self.seq(0, 3), m)
        self.xp = (self.seq(1, 0), m)
        self.xm = (self.seq(3, 0), m)
        self.nxt = ((s + 1) % 16, m)
        self.prv = ((s + 15) % 16, m)

    def mp(self, dy, zl, c):
        return (((self.y + dy) % 4) * 2 + zl) * 2 + c

    def pair(self, dy, zl):
        return ((self.y + dy) % 4) * 2 + zl

    def seq(self, dx, dz):
        return ((self.x + dx) % 4) * 4 + (self.zh + dz) % 4


class Wire:
    def __init__(self, send_sem, recv_sem):
        self.send_sem, self.recv_sem = send_sem, recv_sem
        self.count = 0
        self.open = []

    def send(self, src, dst, to):
        k = self.count
        self.count += 1
        copy = pltpu.make_async_remote_copy(
            src_ref=src,
            dst_ref=dst,
            send_sem=self.send_sem.at[k],
            recv_sem=self.recv_sem.at[k],
            device_id=to,
            device_id_type=MESH,
        )
        copy.start()
        self.open.append(copy)
        return k

    def wait(self, k, landing, frm):
        pltpu.make_async_remote_copy(
            src_ref=landing,
            dst_ref=landing,
            send_sem=self.send_sem.at[k],
            recv_sem=self.recv_sem.at[k],
            device_id=frm,
            device_id_type=MESH,
        ).wait_recv()

    def finish(self):
        for copy in self.open:
            copy.wait_send()


def greet(peers):
    barrier = pltpu.get_barrier_semaphore()
    for peer in peers:
        pl.semaphore_signal(barrier, inc=1, device_id=peer, device_id_type=MESH)
    pl.semaphore_wait(barrier, len(peers))


def gather_mp(w, p, shard, out):
    mine = p.mp(0, p.zl, p.c)
    o = 1 - p.zl
    oc = 1 - p.c
    at = lambda dy, zl, c: out.at[p.mp(dy, zl, c)]
    own = out.at[mine]
    k_y1 = w.send(shard, own, p.yp)
    k_y2 = w.send(shard, own, p.ym)
    k_z = w.send(shard, own, p.zn)
    k_s = w.send(shard, own, p.sib)
    out[mine] = shard[...]
    yield
    w.wait(k_z, at(0, o, p.c), p.zn)
    zb = at(0, o, p.c)
    k_z1 = w.send(zb, zb, p.yp)
    k_z2 = w.send(zb, zb, p.ym)
    k_zs = w.send(zb, zb, p.sib)
    yield
    b = at(3, p.zl, p.c)
    w.wait(k_y1, b, p.ym)
    k_f1 = w.send(b, b, p.yp)
    k_s1 = w.send(b, b, p.sib)
    b = at(1, p.zl, p.c)
    w.wait(k_y2, b, p.yp)
    k_s2 = w.send(b, b, p.sib)
    yield
    b = at(1, o, p.c)
    w.wait(k_z2, b, p.yp)
    k_f2 = w.send(b, b, p.ym)
    k_s3 = w.send(b, b, p.sib)
    b = at(3, o, p.c)
    w.wait(k_z1, b, p.ym)
    k_s4 = w.send(b, b, p.sib)
    yield
    b = at(2, p.zl, p.c)
    w.wait(k_f1, b, p.ym)
    k_s5 = w.send(b, b, p.sib)
    b = at(2, o, p.c)
    w.wait(k_f2, b, p.yp)
    k_s6 = w.send(b, b, p.sib)
    yield
    w.wait(k_s, at(0, p.zl, oc), p.sib)
    w.wait(k_zs, at(0, o, oc), p.sib)
    w.wait(k_s1, at(3, p.zl, oc), p.sib)
    w.wait(k_s2, at(1, p.zl, oc), p.sib)
    w.wait(k_s3, at(1, o, oc), p.sib)
    w.wait(k_s4, at(3, o, oc), p.sib)
    w.wait(k_s5, at(2, p.zl, oc), p.sib)
    w.wait(k_s6, at(2, o, oc), p.sib)


def gather_seq(w, p, shard, out, up):
    mine = p.seq(0, 0)
    at = lambda dx, dz: out.at[p.seq(dx, dz)]
    own = out.at[mine]
    k_zp = w.send(shard, own, p.zp)
    k_zm = w.send(shard, own, p.zm)
    kx = {}
    kx[0] = (w.send(shard, own, p.xp), w.send(shard, own, p.xm))
    out[mine] = shard[...]

    def spread(dz):
        b = at(0, dz)
        kx[dz] = (w.send(b, b, p.xp), w.send(b, b, p.xm))

    kf = {}

    def relay(dz, upward):
        k1, k2 = kx[dz]
        if upward:
            b = at(3, dz)
            w.wait(k1, b, p.xm)
            kf[dz] = (w.send(b, b, p.xp), upward)
            w.wait(k2, at(1, dz), p.xp)
        else:
            b = at(1, dz)
            w.wait(k2, b, p.xp)
            kf[dz] = (w.send(b, b, p.xm), upward)
            w.wait(k1, at(3, dz), p.xm)

    yield
    if up:
        b = at(0, 3)
        w.wait(k_zp, b, p.zm)
        k_zf = w.send(b, b, p.zp)
        spread(3)
        w.wait(k_zm, at(0, 1), p.zp)
        spread(1)
    else:
        b = at(0, 1)
        w.wait(k_zm, b, p.zp)
        k_zf = w.send(b, b, p.zm)
        spread(1)
        w.wait(k_zp, at(0, 3), p.zm)
        spread(3)
    yield
    relay(0, up)
    yield
    w.wait(k_zf, at(0, 2), p.zm if up else p.zp)
    spread(2)
    yield
    relay(3 if up else 1, up)
    yield
    relay(1 if up else 3, not up)
    yield
    relay(2, not up)
    yield
    for dz, (k, upward) in kf.items():
        w.wait(k, at(2, dz), p.xm if upward else p.xp)


def scatter_mp(w, p, part, sibl, acc, land, result):
    o = 1 - p.zl
    ks = {}
    for dy in (2, 1, 3, 0):
        row = ((p.y + dy) % 4) * 2
        ks[dy] = w.send(
            part.at[pl.ds(row, 2), 1 - p.c], sibl.at[pl.ds(row, 2)], p.sib
        )
    yield

    def combine(dy):
        row = ((p.y + dy) % 4) * 2
        w.wait(ks[dy], sibl.at[pl.ds(row, 2)], p.sib)
        for zl in (0, 1):
            acc[row + zl] = (
                part[row + zl, p.c].astype(F32) + sibl[row + zl].astype(F32)
            ).astype(BF16)

    combine(2)
    k0 = w.send(acc.at[p.pair(2, p.zl)], land.at[0], p.yp)
    k1 = w.send(acc.at[p.pair(2, o)], land.at[1], p.ym)
    combine(1)
    k2b = w.send(acc.at[p.pair(1, o)], land.at[2], p.yp)
    combine(3)
    k3a = w.send(acc.at[p.pair(3, p.zl)], land.at[3], p.ym)
    combine(0)
    yield
    w.wait(k0, land.at[0], p.ym)
    i = p.pair(1, p.zl)
    acc[i] = (acc[i].astype(F32) + land[0].astype(F32)).astype(BF16)
    k2a = w.send(acc.at[i], land.at[4], p.yp)
    w.wait(k1, land.at[1], p.yp)
    i = p.pair(3, o)
    acc[i] = (acc[i].astype(F32) + land[1].astype(F32)).astype(BF16)
    k3b = w.send(acc.at[i], land.at[5], p.ym)
    yield
    w.wait(k2b, land.at[2], p.ym)
    w.wait(k3b, land.at[5], p.yp)
    i = p.pair(0, o)
    acc[i] = (acc[i].astype(F32) + land[2].astype(F32) + land[5].astype(F32)).astype(BF16)
    kz = w.send(acc.at[i], land.at[6], p.zn)
    yield
    w.wait(k3a, land.at[3], p.yp)
    w.wait(k2a, land.at[4], p.ym)
    w.wait(kz, land.at[6], p.zn)
    result(
        acc[p.pair(0, p.zl)].astype(F32)
        + land[3].astype(F32)
        + land[4].astype(F32)
        + land[6].astype(F32)
    )


def drain(gens):
    gens = list(gens)
    while gens:
        gens = [g for g in gens if next(g, True) is None]


def k1_body(
    hid, cot, wq, wo, wkv, part,
    q_o, d_o, wq_o, wo_o, wkv_o, emb_o,
    hid_s, cot_s, sibl, acc, land, emb_own, q_land, send_sem, recv_sem,
):
    p = Place()
    w = Wire(send_sem, recv_sem)
    greet((p.sib, p.zn, p.yp, p.ym, p.zp, p.zm, p.xp, p.xm, p.nxt, p.prv))

    def keep(total):
        emb_own[...] = total.astype(BF16)

    ers = scatter_mp(w, p, part, sibl, acc, land, keep)
    gq = gather_seq(w, p, wq, wq_o, True)
    go = gather_seq(w, p, wo, wo_o, False)
    gk = gather_seq(w, p, wkv, wkv_o, True)
    gh = gather_mp(w, p, hid, hid_s)
    gc = gather_mp(w, p, cot, cot_s)
    next(ers)
    next(gq), next(go), next(gk)
    next(ers)
    next(gh), next(gc)
    next(ers)
    next(gq), next(go), next(gk)
    next(ers)
    next(gh), next(gc)
    next(ers, None)
    ea = gather_mp(w, p, emb_own, emb_o)
    next(ea)
    drain([ea, gh, gc, gq, go, gk])

    def project(src, weights, dst):
        def step(b, total):
            return total + jnp.dot(src[b], weights[b], preferred_element_type=F32)

        total = lax.fori_loop(0, 16, step, jnp.zeros((256, 256), F32))
        dst[...] = total.astype(BF16)

    project(hid_s, wq_o, q_o)
    kq = w.send(q_o.at[pl.ds(192, 64)], q_land.at[0], p.prv)
    project(cot_s, wo_o, d_o)
    kd = w.send(d_o.at[pl.ds(192, 64)], q_land.at[1], p.prv)
    w.wait(kq, q_land.at[0], p.nxt)
    w.wait(kd, q_land.at[1], p.nxt)
    w.finish()
    first = lax.broadcasted_iota(jnp.int32, (64, 256), 0) == 0
    for dst, i in ((q_o, 0), (d_o, 1)):
        tail = dst[pl.ds(192, 64), :].astype(F32)
        dst[pl.ds(192, 64), :] = jnp.where(first, tail, q_land[i].astype(F32)).astype(BF16)


def k2_body(part, emb_mine, enc_o, sibl, acc, land, enc_own, send_sem, recv_sem):
    p = Place()
    w = Wire(send_sem, recv_sem)
    greet((p.sib, p.zn, p.yp, p.ym))

    def keep(total):
        v = emb_mine[...].astype(F32) + total
        v = v * lax.rsqrt(jnp.mean(v * v, axis=-1, keepdims=True) + 1e-06)
        enc_own[...] = v.astype(BF16)

    drain([scatter_mp(w, p, part, sibl, acc, land, keep)])
    drain([gather_mp(w, p, enc_own, enc_o)])
    w.finish()


def k3_body(
    attn, dq, wo, wq, out_o, grad_o,
    a_s, a_land, part_o, part_g, sibl_o, sibl_g, acc_o, acc_g, land_o, land_g,
    send_sem, recv_sem,
):
    p = Place()
    w = Wire(send_sem, recv_sem)
    greet((p.sib, p.zn, p.yp, p.ym, p.nxt, p.prv))
    ka = w.send(attn.at[pl.ds(192, 64)], a_land.at[0], p.nxt)
    kd = w.send(dq.at[pl.ds(192, 64)], a_land.at[1], p.nxt)
    first = lax.broadcasted_iota(jnp.int32, (64, 256), 0) == 0
    has_prev = p.s > 0
    for i, (src, k) in enumerate(((attn, ka), (dq, kd))):
        a_s[i, pl.ds(0, 192), :] = src[pl.ds(0, 192), :]
        w.wait(k, a_land.at[i], p.prv)
        got = jnp.where(has_prev, a_land[i].astype(F32), 0.0)
        tail = src[pl.ds(192, 64), :].astype(F32)
        a_s[i, pl.ds(192, 64), :] = jnp.where(first, tail, got).astype(BF16)

    def fill(i, weights, part):
        @pl.loop(0, 8)
        def _(b):
            for c in (0, 1):
                part[b, c] = lax.dot_general(
                    a_s[i], weights[b * 2 + c], (((1,), (1,)), ((), ())),
                    preferred_element_type=F32,
                ).astype(BF16)

    def keep_out(total):
        out_o[...] = total.astype(BF16)

    def keep_grad(total):
        grad_o[...] = total.astype(BF16)

    fill(0, wo, part_o)
    ro = scatter_mp(w, p, part_o, sibl_o, acc_o, land_o, keep_out)
    next(ro)
    fill(1, wq, part_g)
    rg = scatter_mp(w, p, part_g, sibl_g, acc_g, land_g, keep_grad)
    next(rg)
    drain([ro, rg])
    w.finish()


def vmem(n):
    return [pl.BlockSpec(memory_space=pltpu.VMEM)] * n


def call(body, outs, n_in, scratch, messages, cid, name):
    return pl.pallas_call(
        body,
        out_shape=[jax.ShapeDtypeStruct(s, BF16) for s in outs],
        in_specs=vmem(n_in),
        out_specs=vmem(len(outs)),
        scratch_shapes=[pltpu.VMEM(s, BF16) for s in scratch]
        + [pltpu.SemaphoreType.DMA((messages,)), pltpu.SemaphoreType.DMA((messages,))],
        compiler_params=pltpu.CompilerParams(
            collective_id=cid, has_side_effects=True, vmem_limit_bytes=56 * 1024 * 1024
        ),
        name=name,
    )


def rms_rows(values):
    return values * lax.rsqrt(jnp.mean(values * values, axis=-1, keepdims=True) + 1e-06)


def per_device(
    hidden, cotangent, neighbour_ids, neighbour_lengths, embed_table,
    enc_up, enc_down, w_query, w_keyval, w_out,
):
    scale = 128 ** (-0.5)
    vocab_here = embed_table.shape[0]
    local_ids = neighbour_ids.reshape(1024) - lax.axis_index("mp") * vocab_here
    inside = jnp.logical_and(local_ids >= 0, local_ids < vocab_here)
    picked = jnp.take(embed_table, jnp.clip(local_ids, 0, vocab_here - 1), axis=0)
    masked = jnp.where(inside[:, None], picked, jnp.zeros((), picked.dtype))

    hid_r = jnp.roll(hidden, -63, axis=0)
    cot_r = jnp.roll(cotangent, -63, axis=0)
    enc_blk = (64, 896)
    out_blk = (256, 256)
    q, d, wq, wo, wkv, emb = call(
        k1_body,
        [out_blk, out_blk, (16,) + out_blk, (16,) + out_blk, (16, 56, 512), (16,) + enc_blk],
        6,
        [(16,) + out_blk, (16,) + out_blk, (8,) + enc_blk, (8,) + enc_blk, (7,) + enc_blk,
         enc_blk, (2, 64, 256)],
        110, 1, "gathers",
    )(
        hid_r, cot_r, w_query.reshape(256, 256), w_out.reshape(256, 256),
        w_keyval.reshape(56, 512), masked.reshape((8, 2) + enc_blk),
    )
    emb_flat = emb.reshape(1024, 896)
    emb_wide = emb_flat.astype(F32)
    normed = rms_rows(emb_wide).astype(BF16)
    act = jax.nn.gelu(
        lax.dot_general(normed, enc_up, (((1,), (1,)), ((), ())), preferred_element_type=F32)
    ).astype(BF16)
    ffn = jnp.dot(act, enc_down, preferred_element_type=F32).astype(BF16)
    emb_mine = lax.dynamic_index_in_dim(emb, lax.axis_index("mp"), 0, keepdims=False)
    (enc,) = call(
        k2_body,
        [(16,) + enc_blk],
        2,
        [(8,) + enc_blk, (8,) + enc_blk, (7,) + enc_blk, enc_blk],
        30, 2, "ffn_sums",
    )(ffn.reshape((8, 2) + enc_blk), emb_mine)

    keyval = jnp.dot(
        enc.reshape(1024, 896), wkv.reshape(896, 512), preferred_element_type=F32
    ).astype(BF16).reshape(4, 256, 2, 2, 128)
    keys, values = keyval[:, :, :, 0], keyval[:, :, :, 1]
    lens = lax.dynamic_slice_in_dim(neighbour_lengths, lax.axis_index("seq") * 4, 4, 0)
    key_mask = (
        jnp.arange(128, dtype=jnp.int32)[None, None, :] < lens[:, :, None]
    ).reshape(4, 256)
    qg = q.reshape(4, 64, 2, 128)
    dg = d.reshape(4, 64, 2, 128)
    scores = jnp.einsum("gqhd,gkhd->ghqk", qg, keys, preferred_element_type=F32) * scale
    expo = jnp.where(key_mask[:, None, None, :], jnp.exp(scores), 0.0)
    prob = expo / jnp.sum(expo, axis=-1, keepdims=True)
    attn = jnp.einsum(
        "ghqk,gkhd->gqhd", prob.astype(BF16), values, preferred_element_type=F32
    ).astype(BF16)
    d_prob = jnp.einsum("gqhd,gkhd->ghqk", dg, values, preferred_element_type=F32)
    delta = jnp.sum(prob * d_prob, axis=-1, keepdims=True)
    d_score = (prob * (d_prob - delta) * scale).astype(BF16)
    dq = jnp.einsum("ghqk,gkhd->gqhd", d_score, keys, preferred_element_type=F32).astype(BF16)

    big = (8, 2) + out_blk
    out, grad = call(
        k3_body,
        [out_blk, out_blk],
        4,
        [(2,) + out_blk, (2, 64, 256), big, big, (8,) + out_blk, (8,) + out_blk,
         (8,) + out_blk, (8,) + out_blk, (7,) + out_blk, (7,) + out_blk],
        30, 3, "out_sums",
    )(attn.reshape(256, 256), dq.reshape(256, 256), wo, wq)
    return jnp.roll(out, 63, axis=0), jnp.roll(grad, 63, axis=0)


def solution(mesh):
    return jax.shard_map(
        per_device,
        mesh=mesh,
        in_specs=(
            P("seq", "mp"),
            P("seq", "mp"),
            P("seq", None, None),
            P(),
            P("mp", None),
            P("mp", None),
            P("mp", None),
            P("seq", "mp", None),
            P("seq", "mp", None, None),
            P("seq", "mp", None),
        ),
        out_specs=(P("seq", "mp"), P("seq", "mp")),
        check_vma=False,
    )
```

time: 667 us -> 204 us (0.31)
  waiting for transfers between devices: 532 us -> 0 us
  Pallas kernels: 0 us -> 155 us
  blocking collectives: 58.7 us -> 0 us
  matrix products: 25.1 us -> 10.1 us
  between operations: 14.2 us -> 0.84 us
  local copies, waits for them, and re-layouts: 16.6 us -> 25.8 us
    reduce_scatter x3 -> x0, waiting for transfers between devices: 206 us -> none  [the longest x1 72.6 us: per_device(): lax.psum_scatter(out_part, 'mp', scatter_dimension=1, tiled=True)]
    all_gather x5 -> x0, waiting for transfers between devices: 174 us -> none  [the longest x1 57.2 us: per_device(): lax.all_gather(w_out, 'seq', axis=0, tiled=True)]
    pallas_call x0 -> x3, Pallas kernels: none -> 155 us  [the longest x1 82.4 us: per_device(): call(k1_body, [out_blk, out_blk, (16,) + out_blk, (16,) + out_blk, (16, 5...]
    psum x1 -> x0, waiting for transfers between devices: 136 us -> none  [per_device(): total = lax.psum(ffn_part, 'mp')]
    all_gather x1 -> x0, blocking collectives: 58.7 us -> none  [per_device(): lax.all_gather(w_keyval, 'seq', axis=0, tiled=True)]
    dot_general x11 -> x6, matrix products: 25.1 us -> 10.1 us  [the longest x1 4.18 us: per_device(): ffn = jnp.dot(act, enc_down, preferred_element_type=F32).astype(BF16)]
    ppermute x1 -> x0, waiting for transfers between devices: 14.1 us -> none  [from_behind(): return lax.ppermute(shard, axis, pairs)]
    slice x1 -> x9, local copies, waits for them, and re-layouts: 0.8 us -> 8.19 us  [the longest x4 3.34 us: per_device(): return (jnp.roll(out, 63, axis=0), jnp.roll(grad, 63, axis=0))]
  transfers between devices with their start and end apart: 10 -> 0, of which waited for: 10 -> 0; matrix products, arithmetic and copies ran while one was open for 4% -> 0% of each run, Pallas kernels for 0% -> 0%
where the time goes in v1:
time: 204 us; the launch traced here: 202 us
  Pallas kernels  155 us (76%)
  local copies, waits for them, and re-layouts  25.8 us (13%)
  other arithmetic  10.1 us (5%)
  matrix products  10.1 us (5%)
    pallas_call x1, Pallas kernels, per_device(): call(k1_body, [out_blk, out_blk, (16,) + out_blk, (16,) + out_blk, (16, 5...  82.4 us
    pallas_call x1, Pallas kernels, per_device(): call(k3_body, [out_blk, out_blk], 4, [(2,) + out_blk, (2, 64, 256), big,...  39.1 us
    pallas_call x1, Pallas kernels, per_device(): call(k2_body, [(16,) + enc_blk], 2, [(8,) + enc_blk, (8,) + enc_blk, (7,)...  33.8 us
    gather x1, local copies, waits for them, and re-layouts, per_device(): jnp.take(embed_table, jnp.clip(local_ids, 0, vocab_here - 1), axis=0)  8.61 us
    dot_general x1, matrix products, per_device(): ffn = jnp.dot(act, enc_down, preferred_element_type=F32).astype(BF16)  4.18 us

profile of v1, /device:TPU:1, one launch (start us, length us, event | category | flops | bytes accessed | tf_op | source)
XLA Modules:
  0.0 202.2 jit_solution(4496399715535757046)
XLA Ops:
  0.6 0.0 copy-start
  0.7 0.8 constant_dynamic-slice_fusion
  1.5 0.1 copy.20
  1.6 0.1 broadcast_bitcast_fusion
  1.6 0.7 compare_and_fusion.1
  2.3 0.1 and.21
  2.4 0.7 subtract_clamp_fusion
  3.1 0.1 min.16
  3.2 0.8 slice.35
  4.0 0.8 slice.37
  4.8 1.5 reshape.138.wkv
  6.2 0.9 slice.34
  7.1 0.9 slice.36
  8.1 0.7 pad_maximum_fusion
  8.8 1.7 copy_bitcast_fusion.8
  10.5 8.6 %gather_fusion = bf16[1024,896]{1,0:T(8,128)(2,1)S(1)} fusion(bf16[4000,896]{1,0:T(8,128)(2,1)} %param.14, s32[1024]{0:T(1024)S(1)} %broadcast_clamp_fusion), kind=kCustom, calls=%fused_computation | custom fusion | bytes 3674112 | tf_op jit(solution)/shard_map/jit(_take)/gather | solution.py:397
  19.1 1.5 select_select_fusion.part
  20.7 82.4 %gathers.1 = (bf16[256,256]{1,0:T(8,128)(2,1)}, bf16[256,256]{1,0:T(8,128)(2,1)}, bf16[16,256,256]{2,1,0:T(8,128)(2,1)}, bf16[16,256,256]{2,1,0:T(8,128)(2,1)}, ...) custom-call(bf16[256,256]{1,0:T(8,128)(2,1)} %get-tuple-element.22.hid, ...), custom_call_target="tpu_custom_call" | custom-call | tf_op jit(solution)/shard_map/gathers/pallas_call | solution.py:404
  103.1 0.0 copy-start.1
  103.1 2.1 %multiply_reduce_fusion = f32[16,64]{1,0:T(8,128)S(1)} fusion(bf16[16,64,896]{2,1,0:T(8,128)(2,1)} %get-tuple-element.10), kind=kLoop, calls=%fused_computation.4 | loop fusion | flops 2751488 | bytes 1839104 | tf_op jit(solution)/shard_map/reduce_sum | solution.py:386
  105.2 0.1 rsqrt.12
  105.3 0.0 copy-done.1
  105.3 0.7 dynamic-slice_bitcast_fusion.emb_mine
  105.9 0.0 copy-start.7
  105.9 1.6 fusion.1
  107.6 0.0 copy-done
  107.6 0.0 copy-done.7
  107.6 4.2 %convolution_convert_fusion = bf16[1024,896]{1,0:T(8,128)(2,1)} fusion(bf16[224,896]{1,0:T(8,128)(2,1)S(1)} %copy-done, bf16[1024,896]{1,0:T(8,128)(2,1)} %fusion.1, bf16[224,896]{1,0:T(8,128)(2,1)S(1)} %copy-done.7), kind=kOutput, calls=%fused_computation.6 | convolution fusion | flops 825065472 | bytes 4472832 | tf_op jit(solution)/shard_map/dot_general | solution.py:421
  111.8 0.0 copy-start.6
  111.8 33.8 %ffn_sums.1 = bf16[16,64,896]{2,1,0:T(8,128)(2,1)} custom-call(bf16[8,2,64,896]{3,2,1,0:T(8,128)(2,1)} %bitcast.55, bf16[64,896]{1,0:T(8,128)(2,1)} %dynamic-slice_bitcast_fusion.emb_mine), custom_call_target="tpu_custom_call" | custom-call | tf_op jit(solution)/shard_map/ffn_sums/pallas_call | solution.py:423
  145.6 0.0 copy-done.6
  145.6 2.7 %convolution_convert_fusion.1 = bf16[1024,512]{1,0:T(8,128)(2,1)S(1)} fusion(bf16[1024,896]{1,0:T(8,128)(2,1)} %bitcast.54, bf16[896,512]{1,0:T(8,128)(2,1)S(1)} %bitcast.64), kind=kOutput, calls=%fused_computation.7 | convolution fusion | flops 940048384 | bytes 3801088 | tf_op jit(solution)/shard_map/dot_general | solution.py:431
  148.3 0.0 copy-start.4
  148.3 0.0 copy-start.3
  148.3 0.3 reshape.142
  148.6 0.6 copy-done.4
  149.2 0.7 reshape.143
  149.9 0.0 copy-done.3
  149.9 0.7 reshape.145
  150.6 0.0 copy-start.5
  150.6 1.5 fusion.41
  152.1 0.0 copy-done.5
  152.1 0.0 copy-start.2
  152.1 1.1 fusion.6
  153.2 1.5 fusion.10
  154.7 0.0 copy-done.2
  154.7 0.3 fusion.31
  155.0 1.3 fusion.29
  156.4 0.3 fusion.11
  156.7 0.1 copy.25
  156.8 0.7 copy.48
  157.5 0.1 copy.23
  157.7 0.7 copy.49
  158.3 39.1 %out_sums.1 = (bf16[256,256]{1,0:T(8,128)(2,1)}, bf16[256,256]{1,0:T(8,128)(2,1)}) custom-call(bf16[256,256]{1,0:T(8,128)(2,1)} %bitcast.57, bf16[256,256]{1,0:T(8,128)(2,1)} %bitcast.56, bf16[16,256,256]{2,1,0:T(8,128)(2,1)} %get-tuple-element.14.wo, bf16[16,256,256]{2,1,0:T(8,128)(2,1)} %get-tuple-element.15.wq), custom_call_target="tpu_custom_call" | custom-call | tf_op jit(solution)/shard_map/out_sums/pallas_call | solution.py:453
  197.5 0.8 slice.40
  198.3 0.9 slice.41
  199.2 0.7 pad_maximum_fusion.2
  199.9 0.8 slice.42
  200.6 0.9 slice.43
  201.5 0.7 pad_maximum_fusion.3
  (6 shorter events, 0.1 us)
Async XLA Ops:
  0.6 106.9 %copy-start = (bf16[224,896]{1,0:T(8,128)(2,1)S(1)}, bf16[224,896]{1,0:T(8,128)(2,1)}, u32[]{:S(2)}) copy-start(bf16[224,896]{1,0:T(8,128)(2,1)} %param.16) | copy-start | bytes 1204228
  103.1 2.2 %copy-start.1 = (bf16[16,64,896]{2,1,0:T(8,128)(2,1)S(1)}, bf16[16,64,896]{2,1,0:T(8,128)(2,1)}, u32[]{:S(2)}) copy-start(bf16[16,64,896]{2,1,0:T(8,128)(2,1)} %get-tuple-element.10) | copy-start | bytes 5505028
  105.9 1.6 copy-start.7
  111.8 33.8 %copy-start.6 = (bf16[16,56,512]{2,1,0:T(8,128)(2,1)S(1)}, bf16[16,56,512]{2,1,0:T(8,128)(2,1)}, u32[]{:S(2)}) copy-start(bf16[16,56,512]{2,1,0:T(8,128)(2,1)} %get-tuple-element.11) | copy-start | bytes 2752516
  148.3 0.9 copy-start.4
  148.3 1.6 copy-start.3
  150.6 1.5 copy-start.5
  152.1 2.6 %copy-start.2 = (bf16[4,64,2,128]{3,2,1,0:T(2,128)(2,1)S(1)}, bf16[4,64,2,128]{3,2,1,0:T(2,128)(2,1)}, u32[]{:S(2)}) copy-start(bf16[4,64,2,128]{3,2,1,0:T(2,128)(2,1)} %reshape.145) | copy-start | bytes 393220

commit v2 on v1

--- a/solution.py
+++ b/solution.py
@@ -253,212 +253,379 @@
         gens = [g for g in gens if next(g, True) is None]
 
 
-def k1_body(
-    hid, cot, wq, wo, wkv, part,
-    q_o, d_o, wq_o, wo_o, wkv_o, emb_o,
-    hid_s, cot_s, sibl, acc, land, emb_own, q_land, send_sem, recv_sem,
+def gather_pair(w, p, shard, out):
+    o, oc = 1 - p.zl, 1 - p.c
+    mine = p.zl * 2 + p.c
+    k_z = w.send(shard, out.at[mine], p.zn)
+    k_s = w.send(shard, out.at[mine], p.sib)
+    out[mine] = shard[...]
+    yield
+    b = out.at[o * 2 + p.c]
+    w.wait(k_z, b, p.zn)
+    k_zs = w.send(b, b, p.sib)
+    yield
+    w.wait(k_s, out.at[p.zl * 2 + oc], p.sib)
+    w.wait(k_zs, out.at[o * 2 + oc], p.sib)
+
+
+def gather_y(w, p, shard, out):
+    rows = shard.shape[0] // 2
+    lo, hi = pl.ds(0, rows), pl.ds(rows, rows)
+    at = lambda dy: (p.y + dy) % 4
+    own = out.at[at(0)]
+    k1 = w.send(shard, own, p.yp)
+    k2 = w.send(shard, own, p.ym)
+    out[at(0)] = shard[...]
+    yield
+    w.wait(k1, out.at[at(3)], p.ym)
+    b = out.at[at(3), lo]
+    f1 = w.send(b, b, p.yp)
+    w.wait(k2, out.at[at(1)], p.yp)
+    b = out.at[at(1), hi]
+    f2 = w.send(b, b, p.ym)
+    yield
+    w.wait(f1, out.at[at(2), lo], p.ym)
+    w.wait(f2, out.at[at(2), hi], p.yp)
+
+
+def scatter_y(w, p, blk, index, ready, land, result):
+    rows = blk.shape[1] // 2
+    lo, hi = pl.ds(0, rows), pl.ds(rows, rows)
+    i0, i1, i2, i3 = index(0), index(1), index(2), index(3)
+    ready(2)
+    k0 = w.send(blk.at[i2, lo], land.at[0], p.yp)
+    k1 = w.send(blk.at[i2, hi], land.at[1], p.ym)
+    yield
+    ready(1)
+    k2b = w.send(blk.at[i1, hi], land.at[2], p.yp)
+    ready(3)
+    k3a = w.send(blk.at[i3, lo], land.at[3], p.ym)
+    yield
+    w.wait(k0, land.at[0], p.ym)
+    blk[i1, lo, :] = (blk[i1, lo, :].astype(F32) + land[0].astype(F32)).astype(BF16)
+    k2a = w.send(blk.at[i1, lo], land.at[4], p.yp)
+    w.wait(k1, land.at[1], p.yp)
+    blk[i3, hi, :] = (blk[i3, hi, :].astype(F32) + land[1].astype(F32)).astype(BF16)
+    k3b = w.send(blk.at[i3, hi], land.at[5], p.ym)
+    yield
+    ready(0)
+    w.wait(k2b, land.at[2], p.ym)
+    w.wait(k3a, land.at[3], p.yp)
+    w.wait(k2a, land.at[4], p.ym)
+    w.wait(k3b, land.at[5], p.yp)
+    f = lambda v: v.astype(F32)
+    result(lo, f(blk[i0, lo, :]) + f(land[4]) + f(land[3]))
+    result(hi, f(blk[i0, hi, :]) + f(land[2]) + f(land[5]))
+
+
+def scatter_zy(w, p, part, sibl, acc, zland, land, result):
+    o = 1 - p.zl
+    ks, kz = {}, {}
+    for dy in (2, 1, 3, 0):
+        row = ((p.y + dy) % 4) * 2
+        ks[dy] = w.send(
+            part.at[pl.ds(row, 2), 1 - p.c], sibl.at[pl.ds(row, 2)], p.sib
+        )
+    yield
+    for dy in (2, 1, 3, 0):
+        row = ((p.y + dy) % 4) * 2
+        w.wait(ks[dy], sibl.at[pl.ds(row, 2)], p.sib)
+        for zl in (o, p.zl):
+            acc[row + zl] = (
+                part[row + zl, p.c].astype(F32) + sibl[row + zl].astype(F32)
+            ).astype(BF16)
+        kz[dy] = w.send(acc.at[row + o], zland.at[dy], p.zn)
+    yield
+
+    def ready(dy):
+        w.wait(kz[dy], zland.at[dy], p.zn)
+        i = p.pair(dy, p.zl)
+        acc[i] = (acc[i].astype(F32) + zland[dy].astype(F32)).astype(BF16)
+
+    yield from scatter_y(w, p, acc, lambda dy: p.pair(dy, p.zl), ready, land, result)
+
+
+NT = (((1,), (1,)), ((), ()))
+
+
+def body(
+    hid, cot, wq, wo, wkv, table, ids, lens, up, down,
+    out_o, grad_o,
+    tab, idsb, onehot, epart, esib, eacc, eland, emb_own, emb4, normed,
+    up4, down4, fpart, fblk, fland, enc_own, enc,
+    hid_s, cot_s, wq_s, wo_s, wkv_s, wkv_w, wkv_f, kv_s,
+    q_s, d_s, q_land, a_s, a_land,
+    part_o, part_g, sib_o, sib_g, acc_o, acc_g, land_o, zland_g, land_g, sum_o,
+    tab_sem, send_sem, recv_sem,
 ):
     p = Place()
     w = Wire(send_sem, recv_sem)
+    fetch = pltpu.make_async_copy(table, tab.at[pl.ds(0, 4000)], tab_sem)
+    fetch.start()
     greet((p.sib, p.zn, p.yp, p.ym, p.zp, p.zm, p.xp, p.xm, p.nxt, p.prv))
 
-    def keep(total):
-        emb_own[...] = total.astype(BF16)
-
-    ers = scatter_mp(w, p, part, sibl, acc, land, keep)
-    gq = gather_seq(w, p, wq, wq_o, True)
-    go = gather_seq(w, p, wo, wo_o, False)
-    gk = gather_seq(w, p, wkv, wkv_o, True)
     gh = gather_mp(w, p, hid, hid_s)
     gc = gather_mp(w, p, cot, cot_s)
+    gu = gather_pair(w, p, up, up4)
+    gd = gather_pair(w, p, down, down4)
+    gq = gather_seq(w, p, wq, wq_s, True)
+    go = gather_seq(w, p, wo, wo_s, False)
+    gk = gather_seq(w, p, wkv, wkv_s, True)
+    next(gh), next(gc), next(gu), next(gq), next(gd), next(go), next(gk)
+
+    tab[pl.ds(4000, 96), :] = jnp.zeros((96, 896), BF16)
+    cols = jnp.transpose(ids[...] - p.m * 4000)
+    for r in range(8):
+        idsb[r] = jnp.broadcast_to(cols[:, r : r + 1], (128, 128))
+    lane = lax.broadcasted_iota(jnp.int32, (64, 128), 1)
+
+    def lookup(c):
+        def hot(r, _):
+            mine = idsb[r, pl.ds(pl.multiple_of(c * 64, 64), 64), :] - lane
+            rows = pl.ds(pl.multiple_of(r * 64, 64), 64)
+            for k in range(32):
+                onehot[rows, k * 128 : (k + 1) * 128] = jnp.where(
+                    mine == k * 128, 1.0, 0.0
+                ).astype(BF16)
+            return 0
+
+        lax.fori_loop(0, 8, hot, 0)
+
+        def pick(cols_at, width):
+            got = jnp.dot(onehot[...], tab[:, cols_at], preferred_element_type=F32)
+            for r in range(8):
+                epart[r, c, :, cols_at] = got[r * 64 : (r + 1) * 64].astype(BF16)
+
+        def wide(n, _):
+            pick(pl.ds(pl.multiple_of(n * 256, 256), 256), 256)
+            return 0
+
+        lax.fori_loop(0, 3, wide, 0)
+        pick(pl.ds(768, 128), 128)
+
+    def keep_emb(total):
+        emb_own[...] = total.astype(BF16)
+
+    fetch.wait()
+    lookup(1 - p.c)
+    ers = scatter_mp(w, p, epart, esib, eacc, eland, keep_emb)
     next(ers)
-    next(gq), next(go), next(gk)
+    next(gh), next(gc)
+    lookup(p.c)
     next(ers)
     next(gh), next(gc)
     next(ers)
-    next(gq), next(go), next(gk)
+    next(gq)
     next(ers)
     next(gh), next(gc)
     next(ers, None)
-    ea = gather_mp(w, p, emb_own, emb_o)
-    next(ea)
-    drain([ea, gh, gc, gq, go, gk])
+    ey = gather_y(w, p, emb_own, emb4)
+    next(ey)
+    next(gu), next(gq)
+    next(ey)
+    next(gh), next(gc)
+    next(ey, None)
+    e = emb4[...].reshape(256, 896).astype(F32)
+    normed[...] = (
+        e * lax.rsqrt(jnp.mean(e * e, axis=-1, keepdims=True) + 1e-06)
+    ).astype(BF16)
+    next(gd), next(gu, None), next(gd, None)
+
+    def units(j, first):
+        act = jax.nn.gelu(
+            lax.dot_general(normed[...], up4[j], NT, preferred_element_type=F32)
+        ).astype(BF16)
+        got = jnp.dot(act, down4[j], preferred_element_type=F32)
+        if first:
+            fpart[...] = got
+        else:
+            fpart[...] += got
+
+    units(0, True)
+
+    def more(j, _):
+        units(j, False)
+        return 0
+
+    lax.fori_loop(1, 4, more, 0)
+    for y in range(4):
+        fblk[y] = fpart[y * 64 : (y + 1) * 64, :].astype(BF16)
+
+    def keep_enc(rows, total):
+        v = emb_own[rows, :].astype(F32) + total
+        v = v * lax.rsqrt(jnp.mean(v * v, axis=-1, keepdims=True) + 1e-06)
+        enc_own[rows, :] = v.astype(BF16)
+
+    fy = scatter_y(
+        w, p, fblk, lambda dy: (p.y + dy) % 4, lambda dy: None, fland, keep_enc
+    )
+    next(fy)
+    next(fy)
+    next(go)
+    next(fy)
+    next(gk)
+    next(fy, None)
+    ga = gather_mp(w, p, enc_own, enc)
+    next(ga)
+    next(gh, None), next(gc, None)
+    next(gq), next(go), next(gk)
+    next(ga)
+    next(gq), next(go), next(gk)
+    next(ga)
+    next(gq), next(go), next(gk)
+    next(ga)
+    drain([gq])
 
     def project(src, weights, dst):
         def step(b, total):
             return total + jnp.dot(src[b], weights[b], preferred_element_type=F32)
 
         total = lax.fori_loop(0, 16, step, jnp.zeros((256, 256), F32))
-        dst[...] = total.astype(BF16)
-
-    project(hid_s, wq_o, q_o)
-    kq = w.send(q_o.at[pl.ds(192, 64)], q_land.at[0], p.prv)
-    project(cot_s, wo_o, d_o)
-    kd = w.send(d_o.at[pl.ds(192, 64)], q_land.at[1], p.prv)
+        dst[...] = pltpu.roll(total, 193, 0).astype(BF16)
+
+    project(hid_s, wq_s, q_s)
+    kq = w.send(q_s.at[pl.ds(192, 64)], q_land.at[0], p.prv)
+    next(go), next(gk)
+    next(ga)
+    drain([go, gk])
+    project(cot_s, wo_s, d_s)
+    kd = w.send(d_s.at[pl.ds(192, 64)], q_land.at[1], p.prv)
+    for i in range(16):
+        wkv_f[pl.ds(56 * i, 56), :] = wkv_s[i].astype(F32)
+    wkv_w[...] = wkv_f[...].astype(BF16)
+    next(ga, None)
+
+    def keyval(g, _):
+        rows = enc[pl.ds(g * 4, 4)].reshape(256, 896)
+        kv_s[g] = jnp.dot(rows, wkv_w[...], preferred_element_type=F32).astype(BF16)
+        return 0
+
+    lax.fori_loop(0, 4, keyval, 0)
     w.wait(kq, q_land.at[0], p.nxt)
     w.wait(kd, q_land.at[1], p.nxt)
-    w.finish()
+    for copy in w.open:
+        copy.wait_send()
+    w.open = []
     first = lax.broadcasted_iota(jnp.int32, (64, 256), 0) == 0
-    for dst, i in ((q_o, 0), (d_o, 1)):
-        tail = dst[pl.ds(192, 64), :].astype(F32)
-        dst[pl.ds(192, 64), :] = jnp.where(first, tail, q_land[i].astype(F32)).astype(BF16)
-
-
-def k2_body(part, emb_mine, enc_o, sibl, acc, land, enc_own, send_sem, recv_sem):
-    p = Place()
-    w = Wire(send_sem, recv_sem)
-    greet((p.sib, p.zn, p.yp, p.ym))
-
-    def keep(total):
-        v = emb_mine[...].astype(F32) + total
-        v = v * lax.rsqrt(jnp.mean(v * v, axis=-1, keepdims=True) + 1e-06)
-        enc_own[...] = v.astype(BF16)
-
-    drain([scatter_mp(w, p, part, sibl, acc, land, keep)])
-    drain([gather_mp(w, p, enc_own, enc_o)])
-    w.finish()
-
-
-def k3_body(
-    attn, dq, wo, wq, out_o, grad_o,
-    a_s, a_land, part_o, part_g, sibl_o, sibl_g, acc_o, acc_g, land_o, land_g,
-    send_sem, recv_sem,
-):
-    p = Place()
-    w = Wire(send_sem, recv_sem)
-    greet((p.sib, p.zn, p.yp, p.ym, p.nxt, p.prv))
-    ka = w.send(attn.at[pl.ds(192, 64)], a_land.at[0], p.nxt)
-    kd = w.send(dq.at[pl.ds(192, 64)], a_land.at[1], p.nxt)
-    first = lax.broadcasted_iota(jnp.int32, (64, 256), 0) == 0
-    has_prev = p.s > 0
-    for i, (src, k) in enumerate(((attn, ka), (dq, kd))):
-        a_s[i, pl.ds(0, 192), :] = src[pl.ds(0, 192), :]
-        w.wait(k, a_land.at[i], p.prv)
-        got = jnp.where(has_prev, a_land[i].astype(F32), 0.0)
-        tail = src[pl.ds(192, 64), :].astype(F32)
-        a_s[i, pl.ds(192, 64), :] = jnp.where(first, tail, got).astype(BF16)
-
-    def fill(i, weights, part):
+    tail = pl.ds(192, 64)
+    for dst, i in ((q_s, 0), (d_s, 1)):
+        dst[tail, :] = jnp.where(
+            first, dst[tail, :].astype(F32), q_land[i].astype(F32)
+        ).astype(BF16)
+
+    key = lax.broadcasted_iota(jnp.int32, (64, 256), 1)
+    scale = 128 ** (-0.5)
+
+    def attend(g):
+        rows = pl.ds(pl.multiple_of(g * 64, 64), 64)
+        span = p.s * 4 + g
+        live = key < jnp.where(key < 128, lens[span, 0], lens[span, 1] + 128)
+        for h in range(2):
+            head = slice(h * 128, (h + 1) * 128)
+            k = kv_s[g, :, h * 256 : h * 256 + 128]
+            v = kv_s[g, :, h * 256 + 128 : (h + 1) * 256]
+            score = lax.dot_general(q_s[rows, head], k, NT, preferred_element_type=F32)
+            expo = jnp.where(live, jnp.exp(score * scale), 0.0)
+            prob = expo / jnp.sum(expo, axis=-1, keepdims=True)
+            a_s[0, rows, head] = jnp.dot(
+                prob.astype(BF16), v, preferred_element_type=F32
+            ).astype(BF16)
+            d_prob = lax.dot_general(d_s[rows, head], v, NT, preferred_element_type=F32)
+            delta = jnp.sum(prob * d_prob, axis=-1, keepdims=True)
+            d_score = (prob * (d_prob - delta) * scale).astype(BF16)
+            a_s[1, rows, head] = jnp.dot(
+                d_score, k, preferred_element_type=F32
+            ).astype(BF16)
+
+    attend(3)
+    ka = w.send(a_s.at[:, tail], a_land, p.nxt)
+
+    def others(g, _):
+        attend(g)
+        return 0
+
+    lax.fori_loop(0, 3, others, 0)
+    w.wait(ka, a_land, p.prv)
+    for copy in w.open:
+        copy.wait_send()
+    w.open = []
+    for i in range(2):
+        got = jnp.where(p.s > 0, a_land[i].astype(F32), 0.0)
+        a_s[i, tail, :] = jnp.where(first, a_s[i, tail, :].astype(F32), got).astype(BF16)
+
+    def fill(i, weights, part, c):
         @pl.loop(0, 8)
         def _(b):
-            for c in (0, 1):
-                part[b, c] = lax.dot_general(
-                    a_s[i], weights[b * 2 + c], (((1,), (1,)), ((), ())),
-                    preferred_element_type=F32,
-                ).astype(BF16)
+            part[b, c] = lax.dot_general(
+                a_s[i], weights[b * 2 + c], NT, preferred_element_type=F32
+            ).astype(BF16)
 
     def keep_out(total):
-        out_o[...] = total.astype(BF16)
-
-    def keep_grad(total):
-        grad_o[...] = total.astype(BF16)
-
-    fill(0, wo, part_o)
-    ro = scatter_mp(w, p, part_o, sibl_o, acc_o, land_o, keep_out)
+        out_o[...] = pltpu.roll(total, 63, 0).astype(BF16)
+
+    def keep_grad(rows, total):
+        sum_o[rows, :] = total
+
+    ro = scatter_mp(w, p, part_o, sib_o, acc_o, land_o, keep_out)
+    rg = scatter_zy(w, p, part_g, sib_g, acc_g, zland_g, land_g, keep_grad)
+    fill(1, wq_s, part_g, 1 - p.c)
+    next(rg)
+    fill(0, wo_s, part_o, 1 - p.c)
     next(ro)
-    fill(1, wq, part_g)
-    rg = scatter_mp(w, p, part_g, sibl_g, acc_g, land_g, keep_grad)
+    fill(1, wq_s, part_g, p.c)
     next(rg)
-    drain([ro, rg])
+    fill(0, wo_s, part_o, p.c)
+    next(ro)
+    next(rg)
+    next(ro)
+    next(rg)
+    next(ro)
+    next(rg)
+    next(ro, None)
+    next(rg, None)
+    grad_o[...] = pltpu.roll(sum_o[...], 63, 0).astype(BF16)
     w.finish()
-
-
-def vmem(n):
-    return [pl.BlockSpec(memory_space=pltpu.VMEM)] * n
-
-
-def call(body, outs, n_in, scratch, messages, cid, name):
-    return pl.pallas_call(
-        body,
-        out_shape=[jax.ShapeDtypeStruct(s, BF16) for s in outs],
-        in_specs=vmem(n_in),
-        out_specs=vmem(len(outs)),
-        scratch_shapes=[pltpu.VMEM(s, BF16) for s in scratch]
-        + [pltpu.SemaphoreType.DMA((messages,)), pltpu.SemaphoreType.DMA((messages,))],
-        compiler_params=pltpu.CompilerParams(
-            collective_id=cid, has_side_effects=True, vmem_limit_bytes=56 * 1024 * 1024
-        ),
-        name=name,
-    )
-
-
-def rms_rows(values):
-    return values * lax.rsqrt(jnp.mean(values * values, axis=-1, keepdims=True) + 1e-06)
 
 
 def per_device(
     hidden, cotangent, neighbour_ids, neighbour_lengths, embed_table,
     enc_up, enc_down, w_query, w_keyval, w_out,
 ):
-    scale = 128 ** (-0.5)
-    vocab_here = embed_table.shape[0]
-    local_ids = neighbour_ids.reshape(1024) - lax.axis_index("mp") * vocab_here
-    inside = jnp.logical_and(local_ids >= 0, local_ids < vocab_here)
-    picked = jnp.take(embed_table, jnp.clip(local_ids, 0, vocab_here - 1), axis=0)
-    masked = jnp.where(inside[:, None], picked, jnp.zeros((), picked.dtype))
-
-    hid_r = jnp.roll(hidden, -63, axis=0)
-    cot_r = jnp.roll(cotangent, -63, axis=0)
-    enc_blk = (64, 896)
-    out_blk = (256, 256)
-    q, d, wq, wo, wkv, emb = call(
-        k1_body,
-        [out_blk, out_blk, (16,) + out_blk, (16,) + out_blk, (16, 56, 512), (16,) + enc_blk],
-        6,
-        [(16,) + out_blk, (16,) + out_blk, (8,) + enc_blk, (8,) + enc_blk, (7,) + enc_blk,
-         enc_blk, (2, 64, 256)],
-        110, 1, "gathers",
+    blk = (256, 256)
+    row = (64, 896)
+    bf = lambda *s: pltpu.VMEM(s, BF16)
+    vm = pl.BlockSpec(memory_space=pltpu.VMEM)
+    messages = 190
+    out, grad = pl.pallas_call(
+        body,
+        out_shape=[jax.ShapeDtypeStruct(blk, BF16)] * 2,
+        in_specs=[vm] * 5
+        + [pl.BlockSpec(memory_space=pl.ANY), vm, pl.BlockSpec(memory_space=pltpu.SMEM), vm, vm],
+        out_specs=[vm, vm],
+        scratch_shapes=[
+            bf(4096, 896), pltpu.VMEM((8, 128, 128), jnp.int32), bf(512, 4096),
+            bf(8, 2, *row), bf(8, *row), bf(8, *row), bf(7, *row), bf(*row), bf(4, *row),
+            bf(256, 896),
+            bf(4, 224, 896), bf(4, 224, 896), pltpu.VMEM((256, 896), F32), bf(4, *row),
+            bf(6, 32, 896), bf(*row), bf(16, *row),
+            bf(16, *blk), bf(16, *blk), bf(16, *blk), bf(16, *blk), bf(16, 56, 512),
+            bf(896, 512), pltpu.VMEM((896, 512), F32), bf(4, 256, 512),
+            bf(*blk), bf(*blk), bf(2, 64, 256), bf(2, *blk), bf(2, 64, 256),
+            bf(8, 2, *blk), bf(8, 2, *blk), bf(8, *blk), bf(8, *blk), bf(8, *blk), bf(8, *blk),
+            bf(7, *blk), bf(4, *blk), bf(6, 128, 256), pltpu.VMEM(blk, F32),
+            pltpu.SemaphoreType.DMA,
+            pltpu.SemaphoreType.DMA((messages,)), pltpu.SemaphoreType.DMA((messages,)),
+        ],
+        compiler_params=pltpu.CompilerParams(
+            collective_id=1, has_side_effects=True, vmem_limit_bytes=62 * 1024 * 1024
+        ),
+        name="block",
     )(
-        hid_r, cot_r, w_query.reshape(256, 256), w_out.reshape(256, 256),
-        w_keyval.reshape(56, 512), masked.reshape((8, 2) + enc_blk),
+        hidden, cotangent, w_query.reshape(blk), w_out.reshape(blk),
+        w_keyval.reshape(56, 512), embed_table, neighbour_ids.reshape(8, 128),
+        neighbour_lengths, enc_up, enc_down,
     )
-    emb_flat = emb.reshape(1024, 896)
-    emb_wide = emb_flat.astype(F32)
-    normed = rms_rows(emb_wide).astype(BF16)
-    act = jax.nn.gelu(
-        lax.dot_general(normed, enc_up, (((1,), (1,)), ((), ())), preferred_element_type=F32)
-    ).astype(BF16)
-    ffn = jnp.dot(act, enc_down, preferred_element_type=F32).astype(BF16)
-    emb_mine = lax.dynamic_index_in_dim(emb, lax.axis_index("mp"), 0, keepdims=False)
-    (enc,) = call(
-        k2_body,
-        [(16,) + enc_blk],
-        2,
-        [(8,) + enc_blk, (8,) + enc_blk, (7,) + enc_blk, enc_blk],
-        30, 2, "ffn_sums",
-    )(ffn.reshape((8, 2) + enc_blk), emb_mine)
-
-    keyval = jnp.dot(
-        enc.reshape(1024, 896), wkv.reshape(896, 512), preferred_element_type=F32
-    ).astype(BF16).reshape(4, 256, 2, 2, 128)
-    keys, values = keyval[:, :, :, 0], keyval[:, :, :, 1]
-    lens = lax.dynamic_slice_in_dim(neighbour_lengths, lax.axis_index("seq") * 4, 4, 0)
-    key_mask = (
-        jnp.arange(128, dtype=jnp.int32)[None, None, :] < lens[:, :, None]
-    ).reshape(4, 256)
-    qg = q.reshape(4, 64, 2, 128)
-    dg = d.reshape(4, 64, 2, 128)
-    scores = jnp.einsum("gqhd,gkhd->ghqk", qg, keys, preferred_element_type=F32) * scale
-    expo = jnp.where(key_mask[:, None, None, :], jnp.exp(scores), 0.0)
-    prob = expo / jnp.sum(expo, axis=-1, keepdims=True)
-    attn = jnp.einsum(
-        "ghqk,gkhd->gqhd", prob.astype(BF16), values, preferred_element_type=F32
-    ).astype(BF16)
-    d_prob = jnp.einsum("gqhd,gkhd->ghqk", dg, values, preferred_element_type=F32)
-    delta = jnp.sum(prob * d_prob, axis=-1, keepdims=True)
-    d_score = (prob * (d_prob - delta) * scale).astype(BF16)
-    dq = jnp.einsum("ghqk,gkhd->gqhd", d_score, keys, preferred_element_type=F32).astype(BF16)
-
-    big = (8, 2) + out_blk
-    out, grad = call(
-        k3_body,
-        [out_blk, out_blk],
-        4,
-        [(2,) + out_blk, (2, 64, 256), big, big, (8,) + out_blk, (8,) + out_blk,
-         (8,) + out_blk, (8,) + out_blk, (7,) + out_blk, (7,) + out_blk],
-        30, 3, "out_sums",
-    )(attn.reshape(256, 256), dq.reshape(256, 256), wo, wq)
-    return jnp.roll(out, 63, axis=0), jnp.roll(grad, 63, axis=0)
+    return out, grad
 
 
 def solution(mesh):

time: 204 us -> 160 us (0.78)
  local copies, waits for them, and re-layouts: 25.8 us -> 7.68 us
  matrix products: 10.1 us -> 0 us
  other arithmetic: 10.1 us -> 0 us
  Pallas kernels: 155 us -> 149 us
    dot_general x6 -> x0, matrix products: 10.1 us -> none  [the longest x1 4.18 us: per_device(): ffn = jnp.dot(act, enc_down, preferred_element_type=F32).astype(BF16)]
    gather x1 -> x0, local copies, waits for them, and re-layouts: 8.61 us -> none  [per_device(): jnp.take(embed_table, jnp.clip(local_ids, 0, vocab_here - 1), axis=0)]
    slice x9 -> x0, local copies, waits for them, and re-layouts: 8.19 us -> none  [the longest x4 3.34 us: per_device(): return (jnp.roll(out, 63, axis=0), jnp.roll(grad, 63, axis=0))]
    pallas_call x3 -> x1, Pallas kernels: 155 us -> 149 us  [per_device(): pl.pallas_call(body, out_shape=[jax.ShapeDtypeStruct(blk, BF16)] * 2, in_...]
    unnamed x19 -> x3, local copies, waits for them, and re-layouts: 2.05 us -> 4.51 us
    concatenate x3 -> x0, other arithmetic: 2.09 us -> none  [the longest x2 1.37 us: per_device(): return (jnp.roll(out, 63, axis=0), jnp.roll(grad, 63, axis=0))]
    reduce_sum x1 -> x0, other arithmetic: 2.06 us -> none  [rms_rows(): jnp.mean(values * values, axis=-1, keepdims=True) + 1e-06]
where the time goes in v2:
time: 160 us; the launch traced here: 157 us
  Pallas kernels  149 us (93%)
  local copies, waits for them, and re-layouts  7.68 us (5%)
    pallas_call x1, Pallas kernels, per_device(): pl.pallas_call(body, out_shape=[jax.ShapeDtypeStruct(blk, BF16)] * 2, in_...  149 us
    unnamed x3, local copies, waits for them, and re-layouts  4.51 us

profile of v2, /device:TPU:1, one launch (start us, length us, event | category | flops | bytes accessed | tf_op | source)
XLA Modules:
  0.0 157.5 jit_solution(4904521480311683608)
XLA Ops:
  0.6 1.4 copy.12.lens
  2.0 1.5 reshape.18.wkv
  3.5 1.7 %copy_bitcast_fusion = (bf16[256,256]{1,0:T(8,128)(2,1)}, bf16[256,256]{1,0:T(8,128)(2,1)}) fusion(bf16[32,8,2,128]{3,2,1,0:T(2,128)(2,1)} %bitcast.7, bf16[32,8,2,128]{3,2,1,0:T(2,128)(2,1)} %bitcast.8), kind=kLoop, calls=%fused_computation | loop fusion | bytes 524288 | tf_op jit(solution)/shard_map/reshape | solution.py:624
  5.2 149.2 %block.1 = (bf16[256,256]{1,0:T(8,128)(2,1)}, bf16[256,256]{1,0:T(8,128)(2,1)}) custom-call(bf16[256,256]{1,0:T(8,128)(2,1)} %hid.1, bf16[256,256]{1,0:T(8,128)(2,1)} %cot.1, bf16[256,256]{1,0:T(8,128)(2,1)} %get-tuple-element.3.wq, bf16[256,256]{1,0:T(8,128)(2,1)} %get-tuple-element.2.wo, bf16[56,512]{1,0:T(8,128)(2,1)} %reshape.18.wkv, ...), custom_call_target="tpu_custom_call" | custom-call | tf_op jit(solution)/shard_map/block/pallas_call | solution.py:599
  154.3 1.6 copy.19
  155.9 1.6 copy.20

commit v3 on v2

--- a/solution.py
+++ b/solution.py
@@ -21,6 +21,7 @@
         self.y, self.zl, self.c = m // 4, (m // 2) % 2, m % 2
         self.sib = (s, self.mp(0, self.zl, 1 - self.c))
         self.zn = (s, self.mp(0, 1 - self.zl, self.c))
+        self.zo = (self.seq(0, 2 * self.zl + 3), self.mp(0, 1 - self.zl, self.c))
         self.yp = (s, self.mp(1, self.zl, self.c))
         self.ym = (s, self.mp(3, self.zl, self.c))
         self.zp = (self.seq(0, 1), m)
@@ -134,14 +135,70 @@
     w.wait(k_s6, at(2, o, oc), p.sib)
 
 
-def gather_seq(w, p, shard, out, up):
+def scatter_mp(w, p, part, sibl, acc, land, result):
+    o = 1 - p.zl
+    ks = {}
+    for dy in (2, 1, 3, 0):
+        row = ((p.y + dy) % 4) * 2
+        ks[dy] = w.send(
+            part.at[pl.ds(row, 2), 1 - p.c], sibl.at[pl.ds(row, 2)], p.sib
+        )
+    yield
+
+    def combine(dy):
+        row = ((p.y + dy) % 4) * 2
+        w.wait(ks[dy], sibl.at[pl.ds(row, 2)], p.sib)
+        for zl in (0, 1):
+            acc[row + zl] = (
+                part[row + zl, p.c].astype(F32) + sibl[row + zl].astype(F32)
+            ).astype(BF16)
+
+    combine(2)
+    k0 = w.send(acc.at[p.pair(2, p.zl)], land.at[0], p.yp)
+    k1 = w.send(acc.at[p.pair(2, o)], land.at[1], p.ym)
+    combine(1)
+    k2b = w.send(acc.at[p.pair(1, o)], land.at[2], p.yp)
+    combine(3)
+    k3a = w.send(acc.at[p.pair(3, p.zl)], land.at[3], p.ym)
+    combine(0)
+    yield
+    w.wait(k0, land.at[0], p.ym)
+    i = p.pair(1, p.zl)
+    acc[i] = (acc[i].astype(F32) + land[0].astype(F32)).astype(BF16)
+    k2a = w.send(acc.at[i], land.at[4], p.yp)
+    w.wait(k1, land.at[1], p.yp)
+    i = p.pair(3, o)
+    acc[i] = (acc[i].astype(F32) + land[1].astype(F32)).astype(BF16)
+    k3b = w.send(acc.at[i], land.at[5], p.ym)
+    yield
+    w.wait(k2b, land.at[2], p.ym)
+    w.wait(k3b, land.at[5], p.yp)
+    i = p.pair(0, o)
+    acc[i] = (acc[i].astype(F32) + land[2].astype(F32) + land[5].astype(F32)).astype(BF16)
+    kz = w.send(acc.at[i], land.at[6], p.zn)
+    yield
+    w.wait(k3a, land.at[3], p.yp)
+    w.wait(k2a, land.at[4], p.ym)
+    w.wait(kz, land.at[6], p.zn)
+    result(
+        acc[p.pair(0, p.zl)].astype(F32)
+        + land[3].astype(F32)
+        + land[4].astype(F32)
+        + land[6].astype(F32)
+    )
+
+
+def drain(gens):
+    gens = list(gens)
+    while gens:
+        gens = [g for g in gens if next(g, True) is None]
+
+
+def gather_seq(w, p, shard, out, up, late):
     mine = p.seq(0, 0)
     at = lambda dx, dz: out.at[p.seq(dx, dz)]
     own = out.at[mine]
-    k_zp = w.send(shard, own, p.zp)
-    k_zm = w.send(shard, own, p.zm)
-    kx = {}
-    kx[0] = (w.send(shard, own, p.xp), w.send(shard, own, p.xm))
+    kx = {0: (w.send(shard, own, p.xp), w.send(shard, own, p.xm))}
     out[mine] = shard[...]
 
     def spread(dz):
@@ -164,6 +221,15 @@
             w.wait(k1, at(3, dz), p.xm)
 
     yield
+    if late:
+        relay(0, up)
+        yield
+    k_zp = w.send(shard, own, p.zp)
+    k_zm = w.send(shard, own, p.zm)
+    yield
+    if not late:
+        relay(0, up)
+        yield
     if up:
         b = at(0, 3)
         w.wait(k_zp, b, p.zm)
@@ -179,8 +245,6 @@
         w.wait(k_zp, at(0, 3), p.zm)
         spread(3)
     yield
-    relay(0, up)
-    yield
     w.wait(k_zf, at(0, 2), p.zm if up else p.zp)
     spread(2)
     yield
@@ -192,76 +256,17 @@
     yield
     for dz, (k, upward) in kf.items():
         w.wait(k, at(2, dz), p.xm if upward else p.xp)
-
-
-def scatter_mp(w, p, part, sibl, acc, land, result):
-    o = 1 - p.zl
-    ks = {}
-    for dy in (2, 1, 3, 0):
-        row = ((p.y + dy) % 4) * 2
-        ks[dy] = w.send(
-            part.at[pl.ds(row, 2), 1 - p.c], sibl.at[pl.ds(row, 2)], p.sib
-        )
-    yield
-
-    def combine(dy):
-        row = ((p.y + dy) % 4) * 2
-        w.wait(ks[dy], sibl.at[pl.ds(row, 2)], p.sib)
-        for zl in (0, 1):
-            acc[row + zl] = (
-                part[row + zl, p.c].astype(F32) + sibl[row + zl].astype(F32)
-            ).astype(BF16)
-
-    combine(2)
-    k0 = w.send(acc.at[p.pair(2, p.zl)], land.at[0], p.yp)
-    k1 = w.send(acc.at[p.pair(2, o)], land.at[1], p.ym)
-    combine(1)
-    k2b = w.send(acc.at[p.pair(1, o)], land.at[2], p.yp)
-    combine(3)
-    k3a = w.send(acc.at[p.pair(3, p.zl)], land.at[3], p.ym)
-    combine(0)
-    yield
-    w.wait(k0, land.at[0], p.ym)
-    i = p.pair(1, p.zl)
-    acc[i] = (acc[i].astype(F32) + land[0].astype(F32)).astype(BF16)
-    k2a = w.send(acc.at[i], land.at[4], p.yp)
-    w.wait(k1, land.at[1], p.yp)
-    i = p.pair(3, o)
-    acc[i] = (acc[i].astype(F32) + land[1].astype(F32)).astype(BF16)
-    k3b = w.send(acc.at[i], land.at[5], p.ym)
-    yield
-    w.wait(k2b, land.at[2], p.ym)
-    w.wait(k3b, land.at[5], p.yp)
-    i = p.pair(0, o)
-    acc[i] = (acc[i].astype(F32) + land[2].astype(F32) + land[5].astype(F32)).astype(BF16)
-    kz = w.send(acc.at[i], land.at[6], p.zn)
-    yield
-    w.wait(k3a, land.at[3], p.yp)
-    w.wait(k2a, land.at[4], p.ym)
-    w.wait(kz, land.at[6], p.zn)
-    result(
-        acc[p.pair(0, p.zl)].astype(F32)
-        + land[3].astype(F32)
-        + land[4].astype(F32)
-        + land[6].astype(F32)
-    )
-
-
-def drain(gens):
-    gens = list(gens)
-    while gens:
-        gens = [g for g in gens if next(g, True) is None]
 
 
 def gather_pair(w, p, shard, out):
     o, oc = 1 - p.zl, 1 - p.c
     mine = p.zl * 2 + p.c
-    k_z = w.send(shard, out.at[mine], p.zn)
+    k_z = w.send(shard, out.at[mine], p.zo)
     k_s = w.send(shard, out.at[mine], p.sib)
     out[mine] = shard[...]
     yield
     b = out.at[o * 2 + p.c]
-    w.wait(k_z, b, p.zn)
+    w.wait(k_z, b, p.zo)
     k_zs = w.send(b, b, p.sib)
     yield
     w.wait(k_s, out.at[p.zl * 2 + oc], p.sib)
@@ -350,11 +355,11 @@
 
 def body(
     hid, cot, wq, wo, wkv, table, ids, lens, up, down,
-    out_o, grad_o,
+    res,
     tab, idsb, onehot, epart, esib, eacc, eland, emb_own, emb4, normed,
-    up4, down4, fpart, fblk, fland, enc_own, enc,
+    up4, down4, acts, fblk, fland, enc_own, enc,
     hid_s, cot_s, wq_s, wo_s, wkv_s, wkv_w, wkv_f, kv_s,
-    q_s, d_s, q_land, a_s, a_land,
+    q_s, d_s, q_land, last, a_s, a_land,
     part_o, part_g, sib_o, sib_g, acc_o, acc_g, land_o, zland_g, land_g, sum_o,
     tab_sem, send_sem, recv_sem,
 ):
@@ -362,16 +367,17 @@
     w = Wire(send_sem, recv_sem)
     fetch = pltpu.make_async_copy(table, tab.at[pl.ds(0, 4000)], tab_sem)
     fetch.start()
-    greet((p.sib, p.zn, p.yp, p.ym, p.zp, p.zm, p.xp, p.xm, p.nxt, p.prv))
+    greet((p.sib, p.zn, p.zo, p.yp, p.ym, p.zp, p.zm, p.xp, p.xm, p.nxt, p.prv))
 
     gh = gather_mp(w, p, hid, hid_s)
     gc = gather_mp(w, p, cot, cot_s)
     gu = gather_pair(w, p, up, up4)
     gd = gather_pair(w, p, down, down4)
-    gq = gather_seq(w, p, wq, wq_s, True)
-    go = gather_seq(w, p, wo, wo_s, False)
-    gk = gather_seq(w, p, wkv, wkv_s, True)
-    next(gh), next(gc), next(gu), next(gq), next(gd), next(go), next(gk)
+    gq = gather_seq(w, p, wq, wq_s, True, False)
+    go = gather_seq(w, p, wo, wo_s, False, True)
+    gk = gather_seq(w, p, wkv, wkv_s, True, True)
+    next(gh), next(gc), next(gu)
+    next(gq), next(gk), next(go)
 
     tab[pl.ds(4000, 96), :] = jnp.zeros((96, 896), BF16)
     cols = jnp.transpose(ids[...] - p.m * 4000)
@@ -411,45 +417,40 @@
     ers = scatter_mp(w, p, epart, esib, eacc, eland, keep_emb)
     next(ers)
     next(gh), next(gc)
+    next(gq)
     lookup(p.c)
     next(ers)
+    next(gd)
+    next(gq), next(gk), next(go)
+    next(ers)
     next(gh), next(gc)
-    next(ers)
     next(gq)
     next(ers)
+    next(gk), next(go)
     next(gh), next(gc)
     next(ers, None)
     ey = gather_y(w, p, emb_own, emb4)
     next(ey)
-    next(gu), next(gq)
+    next(gu)
     next(ey)
-    next(gh), next(gc)
+    next(gd)
     next(ey, None)
+    next(gu, None), next(gd, None)
+
     e = emb4[...].reshape(256, 896).astype(F32)
     normed[...] = (
         e * lax.rsqrt(jnp.mean(e * e, axis=-1, keepdims=True) + 1e-06)
     ).astype(BF16)
-    next(gd), next(gu, None), next(gd, None)
-
-    def units(j, first):
-        act = jax.nn.gelu(
+    for j in range(4):
+        acts[j] = jax.nn.gelu(
             lax.dot_general(normed[...], up4[j], NT, preferred_element_type=F32)
         ).astype(BF16)
-        got = jnp.dot(act, down4[j], preferred_element_type=F32)
-        if first:
-            fpart[...] = got
-        else:
-            fpart[...] += got
-
-    units(0, True)
-
-    def more(j, _):
-        units(j, False)
-        return 0
-
-    lax.fori_loop(1, 4, more, 0)
+    next(gh), next(gc)
+    total = jnp.dot(acts[0], down4[0], preferred_element_type=F32)
+    for j in range(1, 4):
+        total = total + jnp.dot(acts[j], down4[j], preferred_element_type=F32)
     for y in range(4):
-        fblk[y] = fpart[y * 64 : (y + 1) * 64, :].astype(BF16)
+        fblk[y] = total[y * 64 : (y + 1) * 64, :].astype(BF16)
 
     def keep_enc(rows, total):
         v = emb_own[rows, :].astype(F32) + total
@@ -461,38 +462,47 @@
     )
     next(fy)
     next(fy)
-    next(go)
+    next(gq)
     next(fy)
+    next(gh, None), next(gc, None)
     next(gk)
     next(fy, None)
     ga = gather_mp(w, p, enc_own, enc)
     next(ga)
-    next(gh, None), next(gc, None)
-    next(gq), next(go), next(gk)
+    next(gq), next(go)
     next(ga)
-    next(gq), next(go), next(gk)
+    next(gq)
     next(ga)
-    next(gq), next(go), next(gk)
+    next(gk), next(gq)
     next(ga)
-    drain([gq])
-
-    def project(src, weights, dst):
-        def step(b, total):
-            return total + jnp.dot(src[b], weights[b], preferred_element_type=F32)
-
-        total = lax.fori_loop(0, 16, step, jnp.zeros((256, 256), F32))
-        dst[...] = pltpu.roll(total, 193, 0).astype(BF16)
-
-    project(hid_s, wq_s, q_s)
-    kq = w.send(q_s.at[pl.ds(192, 64)], q_land.at[0], p.prv)
     next(go), next(gk)
     next(ga)
-    drain([go, gk])
-    project(cot_s, wo_s, d_s)
-    kd = w.send(d_s.at[pl.ds(192, 64)], q_land.at[1], p.prv)
+    next(gk), next(go), next(gk)
+    drain([gq])
+
+    def project(src, weights, sums, columns, start):
+        total = None if start else sums[...]
+        for dx in columns:
+            for dz in range(4):
+                b = p.seq(dx, dz)
+                got = jnp.dot(src[b], weights[b], preferred_element_type=F32)
+                total = got if total is None else total + got
+        sums[...] = total
+
+    project(hid_s, wq_s, sum_o, (0, 1, 2, 3), True)
+    q_s[...] = pltpu.roll(sum_o[...], 193, 0).astype(BF16)
+    kq = w.send(q_s.at[pl.ds(192, 64)], q_land.at[0], p.prv)
+    next(go)
+    next(go)
+    project(cot_s, wo_s, sum_o, (0,), True)
+    drain([gk])
     for i in range(16):
         wkv_f[pl.ds(56 * i, 56), :] = wkv_s[i].astype(F32)
     wkv_w[...] = wkv_f[...].astype(BF16)
+    drain([go])
+    project(cot_s, wo_s, sum_o, (1, 3, 2), False)
+    d_s[...] = pltpu.roll(sum_o[...], 193, 0).astype(BF16)
+    kd = w.send(d_s.at[pl.ds(192, 64)], q_land.at[1], p.prv)
     next(ga, None)
 
     def keyval(g, _):
@@ -503,34 +513,33 @@
     lax.fori_loop(0, 4, keyval, 0)
     w.wait(kq, q_land.at[0], p.nxt)
     w.wait(kd, q_land.at[1], p.nxt)
-    for copy in w.open:
-        copy.wait_send()
-    w.open = []
     first = lax.broadcasted_iota(jnp.int32, (64, 256), 0) == 0
     tail = pl.ds(192, 64)
-    for dst, i in ((q_s, 0), (d_s, 1)):
-        dst[tail, :] = jnp.where(
-            first, dst[tail, :].astype(F32), q_land[i].astype(F32)
+    for i, src in ((0, q_s), (1, d_s)):
+        last[i] = jnp.where(
+            first, src[tail, :].astype(F32), q_land[i].astype(F32)
         ).astype(BF16)
 
     key = lax.broadcasted_iota(jnp.int32, (64, 256), 1)
     scale = 128 ** (-0.5)
 
     def attend(g):
-        rows = pl.ds(pl.multiple_of(g * 64, 64), 64)
+        rows = slice(g * 64, (g + 1) * 64)
         span = p.s * 4 + g
-        live = key < jnp.where(key < 128, lens[span, 0], lens[span, 1] + 128)
+        live = key < jnp.where(key < 128, lens[0, span], lens[1, span] + 128)
         for h in range(2):
             head = slice(h * 128, (h + 1) * 128)
             k = kv_s[g, :, h * 256 : h * 256 + 128]
             v = kv_s[g, :, h * 256 + 128 : (h + 1) * 256]
-            score = lax.dot_general(q_s[rows, head], k, NT, preferred_element_type=F32)
+            q = last[0, :, head] if g == 3 else q_s[rows, head]
+            d = last[1, :, head] if g == 3 else d_s[rows, head]
+            score = lax.dot_general(q, k, NT, preferred_element_type=F32)
             expo = jnp.where(live, jnp.exp(score * scale), 0.0)
             prob = expo / jnp.sum(expo, axis=-1, keepdims=True)
             a_s[0, rows, head] = jnp.dot(
                 prob.astype(BF16), v, preferred_element_type=F32
             ).astype(BF16)
-            d_prob = lax.dot_general(d_s[rows, head], v, NT, preferred_element_type=F32)
+            d_prob = lax.dot_general(d, v, NT, preferred_element_type=F32)
             delta = jnp.sum(prob * d_prob, axis=-1, keepdims=True)
             d_score = (prob * (d_prob - delta) * scale).astype(BF16)
             a_s[1, rows, head] = jnp.dot(
@@ -540,28 +549,22 @@
     attend(3)
     ka = w.send(a_s.at[:, tail], a_land, p.nxt)
 
-    def others(g, _):
+    for g in range(3):
         attend(g)
-        return 0
-
-    lax.fori_loop(0, 3, others, 0)
     w.wait(ka, a_land, p.prv)
-    for copy in w.open:
-        copy.wait_send()
-    w.open = []
+    w.open.pop().wait_send()
     for i in range(2):
         got = jnp.where(p.s > 0, a_land[i].astype(F32), 0.0)
         a_s[i, tail, :] = jnp.where(first, a_s[i, tail, :].astype(F32), got).astype(BF16)
 
     def fill(i, weights, part, c):
-        @pl.loop(0, 8)
-        def _(b):
+        for b in range(8):
             part[b, c] = lax.dot_general(
                 a_s[i], weights[b * 2 + c], NT, preferred_element_type=F32
             ).astype(BF16)
 
     def keep_out(total):
-        out_o[...] = pltpu.roll(total, 63, 0).astype(BF16)
+        res[0] = pltpu.roll(total, 63, 0).astype(BF16)
 
     def keep_grad(rows, total):
         sum_o[rows, :] = total
@@ -583,7 +586,7 @@
     next(rg)
     next(ro, None)
     next(rg, None)
-    grad_o[...] = pltpu.roll(sum_o[...], 63, 0).astype(BF16)
+    res[1] = pltpu.roll(sum_o[...], 63, 0).astype(BF16)
     w.finish()
 
 
@@ -595,22 +598,22 @@
     row = (64, 896)
     bf = lambda *s: pltpu.VMEM(s, BF16)
     vm = pl.BlockSpec(memory_space=pltpu.VMEM)
-    messages = 190
-    out, grad = pl.pallas_call(
+    messages = 145
+    res = pl.pallas_call(
         body,
-        out_shape=[jax.ShapeDtypeStruct(blk, BF16)] * 2,
+        out_shape=jax.ShapeDtypeStruct((2,) + blk, BF16),
         in_specs=[vm] * 5
         + [pl.BlockSpec(memory_space=pl.ANY), vm, pl.BlockSpec(memory_space=pltpu.SMEM), vm, vm],
-        out_specs=[vm, vm],
+        out_specs=vm,
         scratch_shapes=[
             bf(4096, 896), pltpu.VMEM((8, 128, 128), jnp.int32), bf(512, 4096),
             bf(8, 2, *row), bf(8, *row), bf(8, *row), bf(7, *row), bf(*row), bf(4, *row),
             bf(256, 896),
-            bf(4, 224, 896), bf(4, 224, 896), pltpu.VMEM((256, 896), F32), bf(4, *row),
+            bf(4, 224, 896), bf(4, 224, 896), bf(4, 256, 224), bf(4, *row),
             bf(6, 32, 896), bf(*row), bf(16, *row),
             bf(16, *blk), bf(16, *blk), bf(16, *blk), bf(16, *blk), bf(16, 56, 512),
             bf(896, 512), pltpu.VMEM((896, 512), F32), bf(4, 256, 512),
-            bf(*blk), bf(*blk), bf(2, 64, 256), bf(2, *blk), bf(2, 64, 256),
+            bf(*blk), bf(*blk), bf(2, 64, 256), bf(2, 64, 256), bf(2, *blk), bf(2, 64, 256),
             bf(8, 2, *blk), bf(8, 2, *blk), bf(8, *blk), bf(8, *blk), bf(8, *blk), bf(8, *blk),
             bf(7, *blk), bf(4, *blk), bf(6, 128, 256), pltpu.VMEM(blk, F32),
             pltpu.SemaphoreType.DMA,
@@ -623,9 +626,9 @@
     )(
         hidden, cotangent, w_query.reshape(blk), w_out.reshape(blk),
         w_keyval.reshape(56, 512), embed_table, neighbour_ids.reshape(8, 128),
-        neighbour_lengths, enc_up, enc_down,
+        neighbour_lengths.T, enc_up, enc_down,
     )
-    return out, grad
+    return res[0], res[1]
 
 
 def solution(mesh):

time: 160 us -> 126 us (0.79); the launches traced: 157 us -> 126 us
  Pallas kernels: 149 us -> 120 us
  local copies, waits for them, and re-layouts: 7.68 us -> 4.86 us
    pallas_call x1, Pallas kernels: 149 us -> 120 us  [per_device(): pl.pallas_call(body, out_shape=jax.ShapeDtypeStruct((2,) + blk, BF16), in...]
    unnamed x3 -> x0, local copies, waits for them, and re-layouts: 4.51 us -> none
    squeeze x0 -> x1, local copies, waits for them, and re-layouts: none -> 1.68 us  [per_device(): return (res[0], res[1])]
where the time goes in v3:
time: 126 us
  Pallas kernels  120 us (95%)
  local copies, waits for them, and re-layouts  4.86 us (4%)
    pallas_call x1, Pallas kernels, per_device(): pl.pallas_call(body, out_shape=jax.ShapeDtypeStruct((2,) + blk, BF16), in...  120 us

profile of v3, /device:TPU:1, one launch (start us, length us, event | category | flops | bytes accessed | tf_op | source)
XLA Modules:
  0.0 125.9 jit_solution(6332745170707101483)
XLA Ops:
  0.6 1.5 %reshape.18.wkv = bf16[56,512]{1,0:T(8,128)(2,1)} reshape(bf16[56,2,2,128]{3,2,1,0:T(2,128)(2,1)} %param.18) | data formatting | bytes 114688 | tf_op jit(solution)/shard_map/reshape | solution.py:628
  2.1 1.7 %copy_bitcast_fusion = (bf16[256,256]{1,0:T(8,128)(2,1)}, bf16[256,256]{1,0:T(8,128)(2,1)}) fusion(bf16[32,8,2,128]{3,2,1,0:T(2,128)(2,1)} %bitcast.12, bf16[32,8,2,128]{3,2,1,0:T(2,128)(2,1)} %bitcast.13), kind=kLoop, calls=%fused_computation | loop fusion | bytes 524288 | tf_op jit(solution)/shard_map/reshape | solution.py:627
  3.8 120.4 %block.1 = bf16[2,256,256]{2,1,0:T(8,128)(2,1)} custom-call(bf16[256,256]{1,0:T(8,128)(2,1)} %hid.1, bf16[256,256]{1,0:T(8,128)(2,1)} %cot.1, bf16[256,256]{1,0:T(8,128)(2,1)} %get-tuple-element.5.wq, bf16[256,256]{1,0:T(8,128)(2,1)} %get-tuple-element.4.wo, bf16[56,512]{1,0:T(8,128)(2,1)} %reshape.18.wkv, bf16[4000,896]{1,0:T(8,128)(2,1)} %table.1, ...), custom_call_target="tpu_custom_call" | custom-call | tf_op jit(solution)/shard_map/block/pallas_call | solution.py:602
  124.2 1.7 %slice_bitcast_fusion = (bf16[256,256]{1,0:T(8,128)(2,1)}, bf16[256,256]{1,0:T(8,128)(2,1)}) fusion(bf16[2,256,256]{2,1,0:T(8,128)(2,1)} %block.1), kind=kLoop, calls=%fused_computation.2 | loop fusion | bytes 524288 | tf_op jit(solution)/shard_map/squeeze | solution.py:631

commit v4 on v3

v4 whole, which is shorter than its diff:
```python
import functools

import jax
import jax.numpy as jnp
from jax import lax
from jax.experimental import pallas as pl
from jax.experimental.pallas import tpu as pltpu
from jax.sharding import PartitionSpec as P

MESH = pl.DeviceIdType.MESH
F32 = jnp.float32
BF16 = jnp.bfloat16


class Place:
    def __init__(self):
        s = lax.axis_index("seq")
        m = lax.axis_index("mp")
        self.s, self.m = s, m
        self.x, self.zh = s // 4, s % 4
        self.y, self.zl, self.c = m // 4, (m // 2) % 2, m % 2
        self.sib = (s, self.mp(0, self.zl, 1 - self.c))
        self.zn = (s, self.mp(0, 1 - self.zl, self.c))
        self.zo = (self.seq(0, 2 * self.zl + 3), self.mp(0, 1 - self.zl, self.c))
        self.yp = (s, self.mp(1, self.zl, self.c))
        self.ym = (s, self.mp(3, self.zl, self.c))
        self.zp = (self.seq(0, 1), m)
        self.zm = (self.seq(0, 3), m)
        self.xp = (self.seq(1, 0), m)
        self.xm = (self.seq(3, 0), m)
        self.nxt = ((s + 1) % 16, m)
        self.prv = ((s + 15) % 16, m)

    def mp(self, dy, zl, c):
        return (((self.y + dy) % 4) * 2 + zl) * 2 + c

    def pair(self, dy, zl):
        return ((self.y + dy) % 4) * 2 + zl

    def seq(self, dx, dz):
        return ((self.x + dx) % 4) * 4 + (self.zh + dz) % 4


class Wire:
    def __init__(self, send_sem, recv_sem):
        self.send_sem, self.recv_sem = send_sem, recv_sem
        self.count = 0
        self.groups = []
        self.open = []

    def slot(self):
        self.count += 1
        return self.count - 1

    def wait(self, k, landing, frm):
        pltpu.make_async_remote_copy(
            src_ref=landing,
            dst_ref=landing,
            send_sem=self.send_sem.at[0],
            recv_sem=self.recv_sem.at[k],
            device_id=frm,
            device_id_type=MESH,
        ).wait_recv()

    def group(self, total):
        return Group(self, total)

    def finish(self):
        for group in list(self.open):
            group.flush()


class Group:
    def __init__(self, wire, total):
        self.wire, self.total = wire, total
        self.sem = wire.send_sem.at[len(wire.groups)]
        wire.groups.append(self)
        wire.open.append(self)

    def send(self, src, dst, to, k=None):
        k = self.wire.slot() if k is None else k
        self.to = to
        pltpu.make_async_remote_copy(
            src_ref=src,
            dst_ref=dst,
            send_sem=self.sem,
            recv_sem=self.wire.recv_sem.at[k],
            device_id=to,
            device_id_type=MESH,
        ).start()
        return k

    def flush(self):
        self.wire.open.remove(self)
        pltpu.make_async_remote_copy(
            src_ref=self.total,
            dst_ref=self.total,
            send_sem=self.sem,
            recv_sem=self.wire.recv_sem.at[0],
            device_id=self.to,
            device_id_type=MESH,
        ).wait_send()


def greet(peers):
    barrier = pltpu.get_barrier_semaphore()
    for peer in peers:
        pl.semaphore_signal(barrier, inc=1, device_id=peer, device_id_type=MESH)
    pl.semaphore_wait(barrier, len(peers))


def gather_mp(w, p, shard, out, flip=False):
    n = w.group(out.at[pl.ds(0, 15)])
    ks = w.slot()
    mine = p.mp(0, p.zl, p.c)
    o = 1 - p.zl
    fore, back, f, b3 = (p.ym, p.yp, 3, 1) if flip else (p.yp, p.ym, 1, 3)
    at = lambda dy, zl, c: out.at[p.mp(dy, zl, c)]
    own = out.at[mine]
    k_y1 = n.send(shard, own, fore)
    k_y2 = n.send(shard, own, back)
    k_z = n.send(shard, own, p.zn)
    n.send(shard, own, p.sib, ks)
    out[mine] = shard[...]
    yield
    w.wait(k_z, at(0, o, p.c), p.zn)
    zb = at(0, o, p.c)
    k_z1 = n.send(zb, zb, fore)
    k_z2 = n.send(zb, zb, back)
    n.send(zb, zb, p.sib, ks)
    yield
    b = at(b3, p.zl, p.c)
    w.wait(k_y1, b, back)
    k_f1 = n.send(b, b, fore)
    n.send(b, b, p.sib, ks)
    b = at(f, p.zl, p.c)
    w.wait(k_y2, b, fore)
    n.send(b, b, p.sib, ks)
    yield
    b = at(f, o, p.c)
    w.wait(k_z2, b, fore)
    k_f2 = n.send(b, b, back)
    n.send(b, b, p.sib, ks)
    b = at(b3, o, p.c)
    w.wait(k_z1, b, back)
    n.send(b, b, p.sib, ks)
    yield
    b = at(2, p.zl, p.c)
    w.wait(k_f1, b, back)
    n.send(b, b, p.sib, ks)
    b = at(2, o, p.c)
    w.wait(k_f2, b, fore)
    n.send(b, b, p.sib, ks)
    yield
    w.wait(ks, out.at[pl.ds(0, 8)], p.sib)


def scatter_mp(w, p, n, part, sibl, acc, land, result, late):
    o = 1 - p.zl
    ks = {}

    def share(dy):
        row = ((p.y + dy) % 4) * 2
        ks[dy] = n.send(
            part.at[pl.ds(row, 2), 1 - p.c], sibl.at[pl.ds(row, 2)], p.sib
        )

    def combine(dy):
        row = ((p.y + dy) % 4) * 2
        w.wait(ks[dy], sibl.at[pl.ds(row, 2)], p.sib)
        for zl in (0, 1):
            acc[row + zl] = (
                part[row + zl, p.c].astype(F32) + sibl[row + zl].astype(F32)
            ).astype(BF16)

    for dy in (2, 1, 3) if late else (2, 1, 3, 0):
        share(dy)
    yield
    combine(2)
    k0 = n.send(acc.at[p.pair(2, p.zl)], land.at[0], p.yp)
    k1 = n.send(acc.at[p.pair(2, o)], land.at[1], p.ym)
    combine(1)
    k2b = n.send(acc.at[p.pair(1, o)], land.at[2], p.yp)
    combine(3)
    k3a = n.send(acc.at[p.pair(3, p.zl)], land.at[3], p.ym)
    yield
    if late:
        share(0)
        yield
    w.wait(k0, land.at[0], p.ym)
    i = p.pair(1, p.zl)
    acc[i] = (acc[i].astype(F32) + land[0].astype(F32)).astype(BF16)
    k2a = n.send(acc.at[i], land.at[4], p.yp)
    w.wait(k1, land.at[1], p.yp)
    i = p.pair(3, o)
    acc[i] = (acc[i].astype(F32) + land[1].astype(F32)).astype(BF16)
    k3b = n.send(acc.at[i], land.at[5], p.ym)
    combine(0)
    yield
    w.wait(k2b, land.at[2], p.ym)
    w.wait(k3b, land.at[5], p.yp)
    i = p.pair(0, o)
    acc[i] = (acc[i].astype(F32) + land[2].astype(F32) + land[5].astype(F32)).astype(BF16)
    kz = n.send(acc.at[i], land.at[6], p.zn)
    yield
    w.wait(k3a, land.at[3], p.yp)
    w.wait(k2a, land.at[4], p.ym)
    w.wait(kz, land.at[6], p.zn)
    result(
        acc[p.pair(0, p.zl)].astype(F32)
        + land[3].astype(F32)
        + land[4].astype(F32)
        + land[6].astype(F32)
    )


def drain(gens):
    gens = list(gens)
    while gens:
        gens = [g for g in gens if next(g, True) is None]


def gather_seq(w, p, shard, out, up, late):
    n = w.group(out.at[pl.ds(0, 15)])
    k_last = w.slot()
    mine = p.seq(0, 0)
    at = lambda dx, dz: out.at[p.seq(dx, dz)]
    own = out.at[mine]
    kx = {0: (n.send(shard, own, p.xp), n.send(shard, own, p.xm))}
    out[mine] = shard[...]

    def spread(dz):
        b = at(0, dz)
        kx[dz] = (n.send(b, b, p.xp), n.send(b, b, p.xm))

    def relay(dz, upward):
        k1, k2 = kx[dz]
        if upward:
            b = at(3, dz)
            w.wait(k1, b, p.xm)
            n.send(b, b, p.xp, k_last)
            w.wait(k2, at(1, dz), p.xp)
        else:
            b = at(1, dz)
            w.wait(k2, b, p.xp)
            n.send(b, b, p.xm, k_last)
            w.wait(k1, at(3, dz), p.xm)

    yield
    if late:
        relay(0, up)
        yield
    k_zp = n.send(shard, own, p.zp)
    k_zm = n.send(shard, own, p.zm)
    yield
    if not late:
        relay(0, up)
        yield
    if up:
        b = at(0, 3)
        w.wait(k_zp, b, p.zm)
        k_zf = n.send(b, b, p.zp)
        spread(3)
        w.wait(k_zm, at(0, 1), p.zp)
        spread(1)
    else:
        b = at(0, 1)
        w.wait(k_zm, b, p.zp)
        k_zf = n.send(b, b, p.zm)
        spread(1)
        w.wait(k_zp, at(0, 3), p.zm)
        spread(3)
    yield
    w.wait(k_zf, at(0, 2), p.zm if up else p.zp)
    spread(2)
    yield
    relay(3 if up else 1, up)
    yield
    relay(1 if up else 3, not up)
    yield
    relay(2, not up)
    yield
    w.wait(k_last, out.at[pl.ds(0, 4)], p.xm)


def gather_pair(w, p, shard, out, other):
    n = w.group(out.at[pl.ds(0, 3)])
    o, oc = 1 - p.zl, 1 - p.c
    mine = p.zl * 2 + p.c
    k_z = n.send(shard, out.at[mine], other)
    k_s = n.send(shard, out.at[mine], p.sib)
    out[mine] = shard[...]
    yield
    b = out.at[o * 2 + p.c]
    w.wait(k_z, b, other)
    k_zs = n.send(b, b, p.sib)
    yield
    w.wait(k_s, out.at[p.zl * 2 + oc], p.sib)
    w.wait(k_zs, out.at[o * 2 + oc], p.sib)


def gather_y(w, p, shard, out):
    n = w.group(out.at[pl.ds(0, 3)])
    rows = shard.shape[0] // 2
    lo, hi = pl.ds(0, rows), pl.ds(rows, rows)
    at = lambda dy: (p.y + dy) % 4
    own = out.at[at(0)]
    k1 = n.send(shard, own, p.yp)
    k2 = n.send(shard, own, p.ym)
    out[at(0)] = shard[...]
    yield
    w.wait(k1, out.at[at(3)], p.ym)
    b = out.at[at(3), lo]
    f1 = n.send(b, b, p.yp)
    w.wait(k2, out.at[at(1)], p.yp)
    b = out.at[at(1), hi]
    f2 = n.send(b, b, p.ym)
    yield
    w.wait(f1, out.at[at(2), lo], p.ym)
    w.wait(f2, out.at[at(2), hi], p.yp)


def scatter_y(w, p, n, blk, index, ready, land, result):
    rows = blk.shape[1] // 2
    lo, hi = pl.ds(0, rows), pl.ds(rows, rows)
    i0, i1, i2, i3 = index(0), index(1), index(2), index(3)
    ready(2)
    k0 = n.send(blk.at[i2, lo], land.at[0], p.yp)
    k1 = n.send(blk.at[i2, hi], land.at[1], p.ym)
    yield
    ready(1)
    k2b = n.send(blk.at[i1, hi], land.at[2], p.yp)
    ready(3)
    k3a = n.send(blk.at[i3, lo], land.at[3], p.ym)
    yield
    w.wait(k0, land.at[0], p.ym)
    blk[i1, lo, :] = (blk[i1, lo, :].astype(F32) + land[0].astype(F32)).astype(BF16)
    k2a = n.send(blk.at[i1, lo], land.at[4], p.yp)
    w.wait(k1, land.at[1], p.yp)
    blk[i3, hi, :] = (blk[i3, hi, :].astype(F32) + land[1].astype(F32)).astype(BF16)
    k3b = n.send(blk.at[i3, hi], land.at[5], p.ym)
    yield
    ready(0)
    w.wait(k2b, land.at[2], p.ym)
    w.wait(k3a, land.at[3], p.yp)
    w.wait(k2a, land.at[4], p.ym)
    w.wait(k3b, land.at[5], p.yp)
    f = lambda v: v.astype(F32)
    result(lo, f(blk[i0, lo, :]) + f(land[4]) + f(land[3]))
    result(hi, f(blk[i0, hi, :]) + f(land[2]) + f(land[5]))


def scatter_zy(w, p, n, part, sibl, acc, zland, land, result):
    o = 1 - p.zl
    ks, kz = {}, {}
    for dy in (2, 1, 3, 0):
        row = ((p.y + dy) % 4) * 2
        ks[dy] = n.send(
            part.at[pl.ds(row, 2), 1 - p.c], sibl.at[pl.ds(row, 2)], p.sib
        )
    yield
    for dy in (2, 1, 3, 0):
        row = ((p.y + dy) % 4) * 2
        w.wait(ks[dy], sibl.at[pl.ds(row, 2)], p.sib)
        for zl in (o, p.zl):
            acc[row + zl] = (
                part[row + zl, p.c].astype(F32) + sibl[row + zl].astype(F32)
            ).astype(BF16)
        kz[dy] = n.send(acc.at[row + o], zland.at[dy], p.zn)
    yield

    def ready(dy):
        w.wait(kz[dy], zland.at[dy], p.zn)
        i = p.pair(dy, p.zl)
        acc[i] = (acc[i].astype(F32) + zland[dy].astype(F32)).astype(BF16)

    yield from scatter_y(w, p, n, acc, lambda dy: p.pair(dy, p.zl), ready, land, result)


NT = (((1,), (1,)), ((), ()))


def body(
    hid, cot, wq, wo, wkv, table, ids, lens, up, down,
    res,
    tab, idsb, onehot, epart, esib, eacc, eland, emb_own, emb4, normed,
    up4, down4, acts, fblk, fland, enc_own, enc,
    hid_s, cot_s, wq_s, wo_s, wkv_s, wkv_w, wkv_f, kv_s,
    q_s, d_s, q_land, last, a_s, a_land,
    part_o, part_g, sib_o, sib_g, acc_o, acc_g, land_o, zland_g, land_g, sum_o, prob_s,
    tab_sem, send_sem, recv_sem,
):
    p = Place()
    w = Wire(send_sem, recv_sem)
    fetch = pltpu.make_async_copy(table, tab.at[pl.ds(0, 4000)], tab_sem)
    fetch.start()
    greet((p.sib, p.zn, p.zo, p.yp, p.ym, p.zp, p.zm, p.xp, p.xm, p.nxt, p.prv))

    gh = gather_mp(w, p, hid, hid_s)
    gc = gather_mp(w, p, cot, cot_s, True)
    gu = gather_pair(w, p, up, up4, p.zo)
    lo, hi = pl.ds(0, 112), pl.ds(112, 112)
    gd = gather_pair(w, p, down.at[lo], down4.at[:, lo], p.zo)
    ge = gather_pair(w, p, down.at[hi], down4.at[:, hi], p.zn)
    gq = gather_seq(w, p, wq, wq_s, True, False)
    gk = gather_seq(w, p, wkv, wkv_s, True, False)
    go = gather_seq(w, p, wo, wo_s, False, True)
    next(gh), next(gc), next(gu)
    next(gq), next(gq)
    next(gk), next(gk)
    next(gd), next(ge), next(go)

    tab[pl.ds(4000, 96), :] = jnp.zeros((96, 896), BF16)
    cols = jnp.transpose(ids[...] - p.m * 4000)
    for r in range(8):
        idsb[r] = jnp.broadcast_to(cols[:, r : r + 1], (128, 128))
    lane = lax.broadcasted_iota(jnp.int32, (64, 128), 1)

    def lookup(c, ys):
        pairs = [p.pair(dy, zl) for dy in ys for zl in (0, 1)]
        high = len(pairs) * 64
        for i, r in enumerate(pairs):
            mine = idsb[r, pl.ds(pl.multiple_of(c * 64, 64), 64), :] - lane
            for k in range(32):
                onehot[i * 64 : (i + 1) * 64, k * 128 : (k + 1) * 128] = jnp.where(
                    mine == k * 128, 1.0, 0.0
                ).astype(BF16)

        def pick(cols_at):
            got = jnp.dot(onehot[0:high, :], tab[:, cols_at], preferred_element_type=F32)
            for i, r in enumerate(pairs):
                epart[r, c, :, cols_at] = got[i * 64 : (i + 1) * 64].astype(BF16)

        for at in (0, 256, 512, 768):
            pick(slice(at, min(at + 256, 896)))

    def keep_emb(total):
        emb_own[...] = total.astype(BF16)

    far = (2, 1, 3)
    fetch.wait()
    lookup(1 - p.c, far)
    ers = scatter_mp(
        w, p, w.group(enc.at[pl.ds(0, 15)]), epart, esib, eacc, eland, keep_emb, True
    )
    next(ers)
    lookup(p.c, far)
    next(ers)
    lookup(1 - p.c, (0,))
    next(ers)
    lookup(p.c, (0,))
    next(ers)
    next(gh), next(gc)
    next(gq), next(gk), next(go)
    next(gu)
    next(ers)
    next(gq), next(gk)
    next(go)
    next(ers, None)
    ey = gather_y(w, p, emb_own, emb4)
    next(ey)
    next(ey)
    next(ey, None)
    next(gu, None)
    next(gq), next(gk)

    e = emb4[...].reshape(256, 896).astype(F32)
    normed[...] = (
        e * lax.rsqrt(jnp.mean(e * e, axis=-1, keepdims=True) + 1e-06)
    ).astype(BF16)
    for j in range(4):
        acts[j] = jax.nn.gelu(
            lax.dot_general(normed[...], up4[j], NT, preferred_element_type=F32)
        ).astype(BF16)
    next(gd), next(ge)
    next(gq), next(gk)
    next(gd, None), next(ge, None)
    total = jnp.dot(acts[0], down4[0], preferred_element_type=F32)
    for j in range(1, 4):
        total = total + jnp.dot(acts[j], down4[j], preferred_element_type=F32)
    for y in range(4):
        fblk[y] = total[y * 64 : (y + 1) * 64, :].astype(BF16)

    def keep_enc(rows, total):
        v = emb_own[rows, :].astype(F32) + total
        v = v * lax.rsqrt(jnp.mean(v * v, axis=-1, keepdims=True) + 1e-06)
        enc_own[rows, :] = v.astype(BF16)

    fy = scatter_y(
        w, p, w.group(enc.at[pl.ds(0, 3)]), fblk, lambda dy: (p.y + dy) % 4, lambda dy: None, fland, keep_enc
    )
    next(fy)
    next(fy)
    next(gq), next(gk)
    next(go)
    next(fy)
    next(gh), next(gh)
    next(gq), next(gk)
    next(fy, None)
    ga = gather_mp(w, p, enc_own, enc)
    next(ga)
    next(go)
    next(ga)
    next(go)
    next(ga)
    next(ga)
    next(gc), next(gc)
    next(go)
    drain([gq, gk])
    for i in range(16):
        wkv_f[pl.ds(56 * i, 56), :] = wkv_s[i].astype(F32)
    wkv_w[...] = wkv_f[...].astype(BF16)
    next(gh)
    next(ga)
    next(go)
    next(gh, None)

    def project(src, weights, sums, columns, start):
        total = None if start else sums[...]
        for dx in columns:
            for dz in range(4):
                b = p.seq(dx, dz)
                got = jnp.dot(src[b], weights[b], preferred_element_type=F32)
                total = got if total is None else total + got
        sums[...] = total

    project(hid_s, wq_s, sum_o, (0, 1, 2, 3), True)
    q_s[...] = pltpu.roll(sum_o[...], 193, 0).astype(BF16)
    next(gc), next(gc, None)
    swap = w.group(q_land)
    kq = swap.send(q_s.at[pl.ds(192, 64)], q_land.at[0], p.prv)
    project(cot_s, wo_s, sum_o, (0,), True)
    drain([go])
    project(cot_s, wo_s, sum_o, (1, 3, 2), False)
    d_s[...] = pltpu.roll(sum_o[...], 193, 0).astype(BF16)
    kd = swap.send(d_s.at[pl.ds(192, 64)], q_land.at[1], p.prv)
    next(ga, None)

    def keyval(g):
        rows = enc[g * 4 : g * 4 + 4].reshape(256, 896)
        kv_s[g] = jnp.dot(rows, wkv_w[...], preferred_element_type=F32).astype(BF16)

    first = lax.broadcasted_iota(jnp.int32, (64, 256), 0) == 0
    tail = pl.ds(192, 64)
    key = lax.broadcasted_iota(jnp.int32, (64, 256), 1)
    scale = 128 ** (-0.5)

    def swapped(i, src):
        last[i] = jnp.where(
            first, src[tail, :].astype(F32), q_land[i].astype(F32)
        ).astype(BF16)

    def heads(spans):
        return [
            (g, h, slice(g * 64, (g + 1) * 64), slice(h * 128, (h + 1) * 128))
            for g in spans
            for h in range(2)
        ]

    def keys_of(g, h):
        return kv_s[g, :, h * 256 : h * 256 + 128]

    def values_of(g, h):
        return kv_s[g, :, h * 256 + 128 : (h + 1) * 256]

    def attend(spans):
        jobs = heads(spans)
        score = [
            lax.dot_general(
                last[0, :, head] if g == 3 else q_s[rows, head], keys_of(g, h), NT,
                preferred_element_type=F32,
            )
            for g, h, rows, head in jobs
        ]
        expo = []
        for (g, _, _, _), x in zip(jobs, score):
            span = p.s * 4 + g
            live = key < jnp.where(key < 128, lens[0, span], lens[1, span] + 128)
            expo.append(jnp.where(live, jnp.exp(x * scale), 0.0))
        prob = [x / jnp.sum(x, axis=-1, keepdims=True) for x in expo]
        attn = [
            jnp.dot(x.astype(BF16), values_of(g, h), preferred_element_type=F32)
            for (g, h, _, _), x in zip(jobs, prob)
        ]
        for (g, h, rows, head), x, y in zip(jobs, prob, attn):
            prob_s[g * 2 + h] = x
            a_s[0, rows, head] = y.astype(BF16)

    def differentiate(spans):
        jobs = heads(spans)
        d_prob = [
            lax.dot_general(
                last[1, :, head] if g == 3 else d_s[rows, head], values_of(g, h), NT,
                preferred_element_type=F32,
            )
            for g, h, rows, head in jobs
        ]
        prob = [prob_s[g * 2 + h] for g, h, _, _ in jobs]
        delta = [jnp.sum(x * y, axis=-1, keepdims=True) for x, y in zip(prob, d_prob)]
        d_score = [
            (x * (y - z) * scale).astype(BF16) for x, y, z in zip(prob, d_prob, delta)
        ]
        d_query = [
            jnp.dot(x, keys_of(g, h), preferred_element_type=F32)
            for (g, h, _, _), x in zip(jobs, d_score)
        ]
        for (_, _, rows, head), y in zip(jobs, d_query):
            a_s[1, rows, head] = y.astype(BF16)

    def give_back(i):
        back = w.group(a_land.at[i])
        return back, back.send(a_s.at[i, tail], a_land.at[i], p.nxt)

    def take_back(i, back, k):
        w.wait(k, a_land.at[i], p.prv)
        back.flush()
        got = jnp.where(p.s > 0, a_land[i].astype(F32), 0.0)
        a_s[i, tail, :] = jnp.where(first, a_s[i, tail, :].astype(F32), got).astype(BF16)

    keyval(3)
    w.wait(kq, q_land.at[0], p.nxt)
    swapped(0, q_s)
    attend((3,))
    back_o = give_back(0)
    for g in range(3):
        keyval(g)
    attend((0, 1, 2))
    w.wait(kd, q_land.at[1], p.nxt)
    swapped(1, d_s)
    differentiate((3,))
    back_g = give_back(1)
    differentiate((0, 1, 2))

    def fill(i, weights, part, c):
        for b in range(8):
            part[b, c] = lax.dot_general(
                a_s[i], weights[b * 2 + c], NT, preferred_element_type=F32
            ).astype(BF16)

    def keep_out(total):
        res[0] = pltpu.roll(total, 63, 0).astype(BF16)

    def keep_grad(rows, total):
        sum_o[rows, :] = total

    blocks = pl.ds(0, 15)
    ro = scatter_mp(
        w, p, w.group(wo_s.at[blocks]), part_o, sib_o, acc_o, land_o, keep_out, False
    )
    rg = scatter_zy(
        w, p, w.group(wq_s.at[blocks]), part_g, sib_g, acc_g, zland_g, land_g, keep_grad
    )
    take_back(0, *back_o)
    fill(0, wo_s, part_o, 1 - p.c)
    next(ro)
    fill(0, wo_s, part_o, p.c)
    next(ro)
    take_back(1, *back_g)
    fill(1, wq_s, part_g, 1 - p.c)
    next(rg)
    fill(1, wq_s, part_g, p.c)
    next(rg)
    next(rg)
    next(ro)
    next(rg)
    next(ro)
    next(rg)
    next(ro, None)
    next(rg, None)
    res[1] = pltpu.roll(sum_o[...], 63, 0).astype(BF16)
    w.finish()


def per_device(
    hidden, cotangent, neighbour_ids, neighbour_lengths, embed_table,
    enc_up, enc_down, w_query, w_keyval, w_out,
):
    blk = (256, 256)
    row = (64, 896)
    bf = lambda *s: pltpu.VMEM(s, BF16)
    vm = pl.BlockSpec(memory_space=pltpu.VMEM)
    messages, groups = 119, 17
    res = pl.pallas_call(
        body,
        out_shape=jax.ShapeDtypeStruct((2,) + blk, BF16),
        in_specs=[vm] * 5
        + [pl.BlockSpec(memory_space=pl.ANY), vm, pl.BlockSpec(memory_space=pltpu.SMEM), vm, vm],
        out_specs=vm,
        scratch_shapes=[
            bf(4096, 896), pltpu.VMEM((8, 128, 128), jnp.int32), bf(512, 4096),
            bf(8, 2, *row), bf(8, *row), bf(8, *row), bf(7, *row), bf(*row), bf(4, *row),
            bf(256, 896),
            bf(4, 224, 896), bf(4, 224, 896), bf(4, 256, 224), bf(4, *row),
            bf(6, 32, 896), bf(*row), bf(16, *row),
            bf(16, *blk), bf(16, *blk), bf(16, *blk), bf(16, *blk), bf(16, 56, 512),
            bf(896, 512), pltpu.VMEM((896, 512), F32), bf(4, 256, 512),
            bf(*blk), bf(*blk), bf(2, 64, 256), bf(2, 64, 256), bf(2, *blk), bf(2, 64, 256),
            bf(8, 2, *blk), bf(8, 2, *blk), bf(8, *blk), bf(8, *blk), bf(8, *blk), bf(8, *blk),
            bf(7, *blk), bf(4, *blk), bf(6, 128, 256), pltpu.VMEM(blk, F32), pltpu.VMEM((8, 64, 256), F32),
            pltpu.SemaphoreType.DMA,
            pltpu.SemaphoreType.DMA((groups,)), pltpu.SemaphoreType.DMA((messages,)),
        ],
        compiler_params=pltpu.CompilerParams(
            collective_id=1, has_side_effects=True, vmem_limit_bytes=62 * 1024 * 1024
        ),
        name="block",
    )(
        hidden, cotangent, w_query.reshape(blk), w_out.reshape(blk),
        w_keyval.reshape(56, 512), embed_table, neighbour_ids.reshape(8, 128),
        neighbour_lengths.T, enc_up, enc_down,
    )
    return res[0], res[1]


def solution(mesh):
    return jax.shard_map(
        per_device,
        mesh=mesh,
        in_specs=(
            P("seq", "mp"),
            P("seq", "mp"),
            P("seq", None, None),
            P(),
            P("mp", None),
            P("mp", None),
            P("mp", None),
            P("seq", "mp", None),
            P("seq", "mp", None, None),
            P("seq", "mp", None),
        ),
        out_specs=(P("seq", "mp"), P("seq", "mp")),
        check_vma=False,
    )
```

time: 126 us -> 110 us (0.87)
  Pallas kernels: 120 us -> 104 us
    pallas_call x1, Pallas kernels: 120 us -> 104 us  [per_device(): pl.pallas_call(body, out_shape=jax.ShapeDtypeStruct((2,) + blk, BF16), in...]
where the time goes in v4:
time: 110 us
  Pallas kernels  104 us (95%)
  local copies, waits for them, and re-layouts  4.86 us (4%)
    pallas_call x1, Pallas kernels, per_device(): pl.pallas_call(body, out_shape=jax.ShapeDtypeStruct((2,) + blk, BF16), in...  104 us

profile of v4, /device:TPU:1, one launch (start us, length us, event | category | flops | bytes accessed | tf_op | source)
XLA Modules:
  0.0 109.6 jit_solution(17983533525631191162)
XLA Ops:
  0.6 1.5 %reshape.18.wkv = bf16[56,512]{1,0:T(8,128)(2,1)} reshape(bf16[56,2,2,128]{3,2,1,0:T(2,128)(2,1)} %param.18) | data formatting | bytes 114688 | tf_op jit(solution)/shard_map/reshape | solution.py:709
  2.1 1.7 %copy_bitcast_fusion = (bf16[256,256]{1,0:T(8,128)(2,1)}, bf16[256,256]{1,0:T(8,128)(2,1)}) fusion(bf16[32,8,2,128]{3,2,1,0:T(2,128)(2,1)} %bitcast.12, bf16[32,8,2,128]{3,2,1,0:T(2,128)(2,1)} %bitcast.13), kind=kLoop, calls=%fused_computation | loop fusion | bytes 524288 | tf_op jit(solution)/shard_map/reshape | solution.py:708
  3.8 104.1 %block.1 = bf16[2,256,256]{2,1,0:T(8,128)(2,1)} custom-call(bf16[256,256]{1,0:T(8,128)(2,1)} %hid.1, bf16[256,256]{1,0:T(8,128)(2,1)} %cot.1, bf16[256,256]{1,0:T(8,128)(2,1)} %get-tuple-element.5.wq, bf16[256,256]{1,0:T(8,128)(2,1)} %get-tuple-element.4.wo, bf16[56,512]{1,0:T(8,128)(2,1)} %reshape.18.wkv, bf16[4000,896]{1,0:T(8,128)(2,1)} %table.1, ...), custom_call_target="tpu_custom_call" | custom-call | tf_op jit(solution)/shard_map/block/pallas_call | solution.py:683
  107.9 1.7 %slice_bitcast_fusion = (bf16[256,256]{1,0:T(8,128)(2,1)}, bf16[256,256]{1,0:T(8,128)(2,1)}) fusion(bf16[2,256,256]{2,1,0:T(8,128)(2,1)} %block.1), kind=kLoop, calls=%fused_computation.2 | loop fusion | bytes 524288 | tf_op jit(solution)/shard_map/squeeze | solution.py:712

commit v5 on v4

--- a/solution.py
+++ b/solution.py
@@ -387,7 +387,8 @@
     up4, down4, acts, fblk, fland, enc_own, enc,
     hid_s, cot_s, wq_s, wo_s, wkv_s, wkv_w, wkv_f, kv_s,
     q_s, d_s, q_land, last, a_s, a_land,
-    part_o, part_g, sib_o, sib_g, acc_o, acc_g, land_o, zland_g, land_g, sum_o, prob_s,
+    part_o, sib_o, acc_o, land_o, part_g, sib_g, acc_g, zland_g, land_g,
+    part_t, sib_t, acc_t, land_t, sum_o, prob_s,
     tab_sem, send_sem, recv_sem,
 ):
     p = Place()
@@ -460,6 +461,7 @@
     ey = gather_y(w, p, emb_own, emb4)
     next(ey)
     next(ey)
+    next(gh), next(gh)
     next(ey, None)
     next(gu, None)
     next(gq), next(gk)
@@ -493,27 +495,25 @@
     next(fy)
     next(gq), next(gk)
     next(go)
+    next(gh)
     next(fy)
-    next(gh), next(gh)
+    next(gc), next(gc)
     next(gq), next(gk)
     next(fy, None)
     ga = gather_mp(w, p, enc_own, enc)
     next(ga)
     next(go)
+    next(gh, None)
     next(ga)
     next(go)
     next(ga)
     next(ga)
-    next(gc), next(gc)
+    next(gc)
     next(go)
     drain([gq, gk])
     for i in range(16):
         wkv_f[pl.ds(56 * i, 56), :] = wkv_s[i].astype(F32)
     wkv_w[...] = wkv_f[...].astype(BF16)
-    next(gh)
-    next(ga)
-    next(go)
-    next(gh, None)
 
     def project(src, weights, sums, columns, start):
         total = None if start else sums[...]
@@ -524,11 +524,13 @@
                 total = got if total is None else total + got
         sums[...] = total
 
+    next(go)
     project(hid_s, wq_s, sum_o, (0, 1, 2, 3), True)
     q_s[...] = pltpu.roll(sum_o[...], 193, 0).astype(BF16)
-    next(gc), next(gc, None)
     swap = w.group(q_land)
     kq = swap.send(q_s.at[pl.ds(192, 64)], q_land.at[0], p.prv)
+    next(ga)
+    next(gc, None)
     project(cot_s, wo_s, sum_o, (0,), True)
     drain([go])
     project(cot_s, wo_s, sum_o, (1, 3, 2), False)
@@ -624,49 +626,64 @@
     back_o = give_back(0)
     for g in range(3):
         keyval(g)
+    def fill(i, weights, part, c, rows):
+        for b in range(8):
+            part[b, c] = lax.dot_general(
+                a_s[i, rows, :], weights[b * 2 + c], NT, preferred_element_type=F32
+            ).astype(BF16)
+
+    def keep_out(total):
+        res[0] = pltpu.roll(total, 63, 0).astype(BF16)
+
+    def keep_head(rows, total):
+        sum_o[rows, :] = total
+
+    def keep_tail(total):
+        sum_o[tail, :] = total
+
+    blocks = pl.ds(0, 15)
+    body_rows, every = pl.ds(0, 192), slice(None)
+    ro = scatter_mp(
+        w, p, w.group(wo_s.at[blocks]), part_o, sib_o, acc_o, land_o, keep_out, False
+    )
+    rg = scatter_zy(
+        w, p, w.group(wq_s.at[blocks, body_rows]),
+        part_g, sib_g, acc_g, zland_g, land_g, keep_head,
+    )
+    rt = scatter_mp(
+        w, p, w.group(wq_s.at[blocks, pl.ds(0, 64)]),
+        part_t, sib_t, acc_t, land_t, keep_tail, False,
+    )
     attend((0, 1, 2))
+    differentiate((0, 1, 2))
+    fill(1, wq_s, part_g, 1 - p.c, body_rows)
+    next(rg)
     w.wait(kd, q_land.at[1], p.nxt)
     swapped(1, d_s)
     differentiate((3,))
     back_g = give_back(1)
-    differentiate((0, 1, 2))
-
-    def fill(i, weights, part, c):
-        for b in range(8):
-            part[b, c] = lax.dot_general(
-                a_s[i], weights[b * 2 + c], NT, preferred_element_type=F32
-            ).astype(BF16)
-
-    def keep_out(total):
-        res[0] = pltpu.roll(total, 63, 0).astype(BF16)
-
-    def keep_grad(rows, total):
-        sum_o[rows, :] = total
-
-    blocks = pl.ds(0, 15)
-    ro = scatter_mp(
-        w, p, w.group(wo_s.at[blocks]), part_o, sib_o, acc_o, land_o, keep_out, False
-    )
-    rg = scatter_zy(
-        w, p, w.group(wq_s.at[blocks]), part_g, sib_g, acc_g, zland_g, land_g, keep_grad
-    )
+    fill(1, wq_s, part_g, p.c, body_rows)
+    next(rg)
     take_back(0, *back_o)
-    fill(0, wo_s, part_o, 1 - p.c)
+    fill(0, wo_s, part_o, 1 - p.c, every)
     next(ro)
-    fill(0, wo_s, part_o, p.c)
+    fill(0, wo_s, part_o, p.c, every)
     next(ro)
+    next(rg)
     take_back(1, *back_g)
-    fill(1, wq_s, part_g, 1 - p.c)
-    next(rg)
-    fill(1, wq_s, part_g, p.c)
-    next(rg)
+    fill(1, wq_s, part_t, 1 - p.c, tail)
+    next(rt)
+    fill(1, wq_s, part_t, p.c, tail)
+    next(rt)
     next(rg)
     next(ro)
+    next(rt)
     next(rg)
     next(ro)
-    next(rg)
+    next(rt)
+    next(rg, None)
     next(ro, None)
-    next(rg, None)
+    next(rt, None)
     res[1] = pltpu.roll(sum_o[...], 63, 0).astype(BF16)
     w.finish()
 
@@ -679,7 +696,7 @@
     row = (64, 896)
     bf = lambda *s: pltpu.VMEM(s, BF16)
     vm = pl.BlockSpec(memory_space=pltpu.VMEM)
-    messages, groups = 119, 17
+    messages, groups = 130, 18
     res = pl.pallas_call(
         body,
         out_shape=jax.ShapeDtypeStruct((2,) + blk, BF16),
@@ -695,8 +712,10 @@
             bf(16, *blk), bf(16, *blk), bf(16, *blk), bf(16, *blk), bf(16, 56, 512),
             bf(896, 512), pltpu.VMEM((896, 512), F32), bf(4, 256, 512),
             bf(*blk), bf(*blk), bf(2, 64, 256), bf(2, 64, 256), bf(2, *blk), bf(2, 64, 256),
-            bf(8, 2, *blk), bf(8, 2, *blk), bf(8, *blk), bf(8, *blk), bf(8, *blk), bf(8, *blk),
-            bf(7, *blk), bf(4, *blk), bf(6, 128, 256), pltpu.VMEM(blk, F32), pltpu.VMEM((8, 64, 256), F32),
+            bf(8, 2, *blk), bf(8, *blk), bf(8, *blk), bf(7, *blk),
+            bf(8, 2, 192, 256), bf(8, 192, 256), bf(8, 192, 256), bf(4, 192, 256), bf(6, 96, 256),
+            bf(8, 2, 64, 256), bf(8, 64, 256), bf(8, 64, 256), bf(7, 64, 256),
+            pltpu.VMEM(blk, F32), pltpu.VMEM((8, 64, 256), F32),
             pltpu.SemaphoreType.DMA,
             pltpu.SemaphoreType.DMA((groups,)), pltpu.SemaphoreType.DMA((messages,)),
         ],

time: 110 us -> 106 us (0.964); the launches traced: 110 us -> 104 us
  Pallas kernels: 104 us -> 98.4 us
    pallas_call x1, Pallas kernels: 104 us -> 98.4 us  [per_device(): pl.pallas_call(body, out_shape=jax.ShapeDtypeStruct((2,) + blk, BF16), in...]
where the time goes in v5:
time: 106 us; the launch traced here: 104 us
  Pallas kernels  98.4 us (93%)
  local copies, waits for them, and re-layouts  4.86 us (5%)
    pallas_call x1, Pallas kernels, per_device(): pl.pallas_call(body, out_shape=jax.ShapeDtypeStruct((2,) + blk, BF16), in...  98.4 us

profile of v5, /device:TPU:1, one launch (start us, length us, event | category | flops | bytes accessed | tf_op | source)
XLA Modules:
  0.0 103.9 jit_solution(983485970155687619)
XLA Ops:
  0.6 1.5 %reshape.18.wkv = bf16[56,512]{1,0:T(8,128)(2,1)} reshape(bf16[56,2,2,128]{3,2,1,0:T(2,128)(2,1)} %param.18) | data formatting | bytes 114688 | tf_op jit(solution)/shard_map/reshape | solution.py:728
  2.1 1.7 %copy_bitcast_fusion = (bf16[256,256]{1,0:T(8,128)(2,1)}, bf16[256,256]{1,0:T(8,128)(2,1)}) fusion(bf16[32,8,2,128]{3,2,1,0:T(2,128)(2,1)} %bitcast.12, bf16[32,8,2,128]{3,2,1,0:T(2,128)(2,1)} %bitcast.13), kind=kLoop, calls=%fused_computation | loop fusion | bytes 524288 | tf_op jit(solution)/shard_map/reshape | solution.py:727
  3.8 98.4 %block.1 = bf16[2,256,256]{2,1,0:T(8,128)(2,1)} custom-call(bf16[256,256]{1,0:T(8,128)(2,1)} %hid.1, bf16[256,256]{1,0:T(8,128)(2,1)} %cot.1, bf16[256,256]{1,0:T(8,128)(2,1)} %get-tuple-element.5.wq, bf16[256,256]{1,0:T(8,128)(2,1)} %get-tuple-element.4.wo, bf16[56,512]{1,0:T(8,128)(2,1)} %reshape.18.wkv, bf16[4000,896]{1,0:T(8,128)(2,1)} %table.1, ...), custom_call_target="tpu_custom_call" | custom-call | tf_op jit(solution)/shard_map/block/pallas_call | solution.py:700
  102.2 1.7 %slice_bitcast_fusion = (bf16[256,256]{1,0:T(8,128)(2,1)}, bf16[256,256]{1,0:T(8,128)(2,1)}) fusion(bf16[2,256,256]{2,1,0:T(8,128)(2,1)} %block.1), kind=kLoop, calls=%fused_computation.2 | loop fusion | bytes 524288 | tf_op jit(solution)/shard_map/squeeze | solution.py:731

commit v6 on v5

--- a/solution.py
+++ b/solution.py
@@ -223,8 +223,11 @@
 def gather_seq(w, p, shard, out, up, late):
     n = w.group(out.at[pl.ds(0, 15)])
     k_last = w.slot()
+    away = {0: 0, "behind": 3 - 2 * p.zl, "ahead": 1 + 2 * p.zl, 2: 2}
+    ahead = (p.seq(0, away["ahead"]), p.m)
+    behind = (p.seq(0, away["behind"]), p.m)
     mine = p.seq(0, 0)
-    at = lambda dx, dz: out.at[p.seq(dx, dz)]
+    at = lambda dx, dz: out.at[p.seq(dx, away[dz])]
     own = out.at[mine]
     kx = {0: (n.send(shard, own, p.xp), n.send(shard, own, p.xm))}
     out[mine] = shard[...]
@@ -250,33 +253,25 @@
     if late:
         relay(0, up)
         yield
-    k_zp = n.send(shard, own, p.zp)
-    k_zm = n.send(shard, own, p.zm)
+    k_a = n.send(shard, own, ahead)
+    k_b = n.send(shard, own, behind)
     yield
     if not late:
         relay(0, up)
         yield
-    if up:
-        b = at(0, 3)
-        w.wait(k_zp, b, p.zm)
-        k_zf = n.send(b, b, p.zp)
-        spread(3)
-        w.wait(k_zm, at(0, 1), p.zp)
-        spread(1)
-    else:
-        b = at(0, 1)
-        w.wait(k_zm, b, p.zp)
-        k_zf = n.send(b, b, p.zm)
-        spread(1)
-        w.wait(k_zp, at(0, 3), p.zm)
-        spread(3)
-    yield
-    w.wait(k_zf, at(0, 2), p.zm if up else p.zp)
+    b = at(0, "behind")
+    w.wait(k_a, b, behind)
+    k_zf = n.send(b, b, ahead)
+    spread("behind")
+    w.wait(k_b, at(0, "ahead"), ahead)
+    spread("ahead")
+    yield
+    w.wait(k_zf, at(0, 2), behind)
     spread(2)
     yield
-    relay(3 if up else 1, up)
-    yield
-    relay(1 if up else 3, not up)
+    relay("behind", up)
+    yield
+    relay("ahead", not up)
     yield
     relay(2, not up)
     yield
@@ -304,18 +299,21 @@
     rows = shard.shape[0] // 2
     lo, hi = pl.ds(0, rows), pl.ds(rows, rows)
     at = lambda dy: (p.y + dy) % 4
-    own = out.at[at(0)]
-    k1 = n.send(shard, own, p.yp)
-    k2 = n.send(shard, own, p.ym)
+    k1 = n.send(shard.at[lo], out.at[at(0), lo], p.yp)
+    k2 = n.send(shard.at[hi], out.at[at(0), hi], p.ym)
+    k3 = n.send(shard.at[hi], out.at[at(0), hi], p.yp)
+    k4 = n.send(shard.at[lo], out.at[at(0), lo], p.ym)
     out[at(0)] = shard[...]
     yield
-    w.wait(k1, out.at[at(3)], p.ym)
     b = out.at[at(3), lo]
+    w.wait(k1, b, p.ym)
     f1 = n.send(b, b, p.yp)
-    w.wait(k2, out.at[at(1)], p.yp)
     b = out.at[at(1), hi]
+    w.wait(k2, b, p.yp)
     f2 = n.send(b, b, p.ym)
     yield
+    w.wait(k3, out.at[at(3), hi], p.ym)
+    w.wait(k4, out.at[at(1), lo], p.yp)
     w.wait(f1, out.at[at(2), lo], p.ym)
     w.wait(f2, out.at[at(2), hi], p.yp)
 
@@ -696,7 +694,7 @@
     row = (64, 896)
     bf = lambda *s: pltpu.VMEM(s, BF16)
     vm = pl.BlockSpec(memory_space=pltpu.VMEM)
-    messages, groups = 130, 18
+    messages, groups = 132, 18
     res = pl.pallas_call(
         body,
         out_shape=jax.ShapeDtypeStruct((2,) + blk, BF16),

time: 106 us -> 104 us (0.981); the launches traced: 104 us -> 104 us
  no operation moved by 1% of the time
where the time goes in v6:
time: 104 us
  Pallas kernels  98.6 us (95%)
  local copies, waits for them, and re-layouts  4.86 us (5%)
    pallas_call x1, Pallas kernels, per_device(): pl.pallas_call(body, out_shape=jax.ShapeDtypeStruct((2,) + blk, BF16), in...  98.6 us

profile of v6, /device:TPU:1, one launch (start us, length us, event | category | flops | bytes accessed | tf_op | source)
XLA Modules:
  0.0 104.1 jit_solution(9566381507700366057)
XLA Ops:
  0.6 1.5 %reshape.18.wkv = bf16[56,512]{1,0:T(8,128)(2,1)} reshape(bf16[56,2,2,128]{3,2,1,0:T(2,128)(2,1)} %param.18) | data formatting | bytes 114688 | tf_op jit(solution)/shard_map/reshape | solution.py:726
  2.1 1.7 %copy_bitcast_fusion = (bf16[256,256]{1,0:T(8,128)(2,1)}, bf16[256,256]{1,0:T(8,128)(2,1)}) fusion(bf16[32,8,2,128]{3,2,1,0:T(2,128)(2,1)} %bitcast.12, bf16[32,8,2,128]{3,2,1,0:T(2,128)(2,1)} %bitcast.13), kind=kLoop, calls=%fused_computation | loop fusion | bytes 524288 | tf_op jit(solution)/shard_map/reshape | solution.py:725
  3.8 98.6 %block.1 = bf16[2,256,256]{2,1,0:T(8,128)(2,1)} custom-call(bf16[256,256]{1,0:T(8,128)(2,1)} %hid.1, bf16[256,256]{1,0:T(8,128)(2,1)} %cot.1, bf16[256,256]{1,0:T(8,128)(2,1)} %get-tuple-element.5.wq, bf16[256,256]{1,0:T(8,128)(2,1)} %get-tuple-element.4.wo, bf16[56,512]{1,0:T(8,128)(2,1)} %reshape.18.wkv, bf16[4000,896]{1,0:T(8,128)(2,1)} %table.1, ...), custom_call_target="tpu_custom_call" | custom-call | tf_op jit(solution)/shard_map/block/pallas_call | solution.py:698
  102.4 1.7 %slice_bitcast_fusion = (bf16[256,256]{1,0:T(8,128)(2,1)}, bf16[256,256]{1,0:T(8,128)(2,1)}) fusion(bf16[2,256,256]{2,1,0:T(8,128)(2,1)} %block.1), kind=kLoop, calls=%fused_computation.2 | loop fusion | bytes 524288 | tf_op jit(solution)/shard_map/squeeze | solution.py:729

commit v7 on v6

--- a/solution.py
+++ b/solution.py
@@ -102,10 +102,11 @@
         ).wait_send()
 
 
-def greet(peers):
+def greet(peers, meanwhile):
     barrier = pltpu.get_barrier_semaphore()
     for peer in peers:
         pl.semaphore_signal(barrier, inc=1, device_id=peer, device_id_type=MESH)
+    meanwhile()
     pl.semaphore_wait(barrier, len(peers))
 
 
@@ -379,7 +380,7 @@
 
 
 def body(
-    hid, cot, wq, wo, wkv, table, ids, lens, up, down,
+    hid, cot, wq3, wo3, wkv3, table, ids, lens, up, down,
     res,
     tab, idsb, onehot, epart, esib, eacc, eland, emb_own, emb4, normed,
     up4, down4, acts, fblk, fland, enc_own, enc,
@@ -387,13 +388,21 @@
     q_s, d_s, q_land, last, a_s, a_land,
     part_o, sib_o, acc_o, land_o, part_g, sib_g, acc_g, zland_g, land_g,
     part_t, sib_t, acc_t, land_t, sum_o, prob_s,
-    tab_sem, send_sem, recv_sem,
+    wq, wo, wkv, tab_sem, send_sem, recv_sem,
 ):
     p = Place()
     w = Wire(send_sem, recv_sem)
     fetch = pltpu.make_async_copy(table, tab.at[pl.ds(0, 4000)], tab_sem)
     fetch.start()
-    greet((p.sib, p.zn, p.zo, p.yp, p.ym, p.zp, p.zm, p.xp, p.xm, p.nxt, p.prv))
+    def relay_weights():
+        for h in range(2):
+            head = slice(h * 128, (h + 1) * 128)
+            wq[:, head] = wq3[:, h, :]
+            wo[:, head] = wo3[:, h, :]
+            for kv in range(2):
+                wkv[:, h * 256 + kv * 128 : h * 256 + (kv + 1) * 128] = wkv3[:, h, kv, :]
+
+    greet((p.sib, p.zn, p.zo, p.yp, p.ym, p.zp, p.zm, p.xp, p.xm, p.nxt, p.prv), relay_weights)
 
     gh = gather_mp(w, p, hid, hid_s)
     gc = gather_mp(w, p, cot, cot_s, True)
@@ -714,6 +723,7 @@
             bf(8, 2, 192, 256), bf(8, 192, 256), bf(8, 192, 256), bf(4, 192, 256), bf(6, 96, 256),
             bf(8, 2, 64, 256), bf(8, 64, 256), bf(8, 64, 256), bf(7, 64, 256),
             pltpu.VMEM(blk, F32), pltpu.VMEM((8, 64, 256), F32),
+            bf(*blk), bf(*blk), bf(56, 512),
             pltpu.SemaphoreType.DMA,
             pltpu.SemaphoreType.DMA((groups,)), pltpu.SemaphoreType.DMA((messages,)),
         ],
@@ -722,8 +732,7 @@
         ),
         name="block",
     )(
-        hidden, cotangent, w_query.reshape(blk), w_out.reshape(blk),
-        w_keyval.reshape(56, 512), embed_table, neighbour_ids.reshape(8, 128),
+        hidden, cotangent, w_query, w_out, w_keyval, embed_table, neighbour_ids.reshape(8, 128),
         neighbour_lengths.T, enc_up, enc_down,
     )
     return res[0], res[1]

time: 104 us -> 101 us (0.971)
  local copies, waits for them, and re-layouts: 4.86 us -> 1.68 us
    reshape x2 -> x0, local copies, waits for them, and re-layouts: 3.17 us -> none  [the longest x1 1.7 us: per_device(): w_out.reshape(blk)]
where the time goes in v7:
time: 101 us
  Pallas kernels  98.9 us (98%)
  local copies, waits for them, and re-layouts  1.68 us (2%)
    pallas_call x1, Pallas kernels, per_device(): pl.pallas_call(body, out_shape=jax.ShapeDtypeStruct((2,) + blk, BF16), in...  98.9 us

profile of v7, /device:TPU:1, one launch (start us, length us, event | category | flops | bytes accessed | tf_op | source)
XLA Modules:
  0.0 101.2 jit_solution(1873614644651707842)
XLA Ops:
  0.6 98.9 %block.1 = bf16[2,256,256]{2,1,0:T(8,128)(2,1)} custom-call(bf16[256,256]{1,0:T(8,128)(2,1)} %hid.1, bf16[256,256]{1,0:T(8,128)(2,1)} %cot.1, bf16[256,2,128]{2,1,0:T(2,128)(2,1)} %wq3.1, bf16[256,2,128]{2,1,0:T(2,128)(2,1)} %wo3.1, bf16[56,2,2,128]{3,2,1,0:T(2,128)(2,1)} %wkv3.1, bf16[4000,896]{1,0:T(8,128)(2,1)} %table.1, s32[8,128]{1,0:T(8,128)} %bitcast.6, ...), custom_call_target="tpu_custom_call" | custom-call | tf_op jit(solution)/shard_map/block/pallas_call | solution.py:707
  99.5 1.7 %slice_bitcast_fusion = (bf16[256,256]{1,0:T(8,128)(2,1)}, bf16[256,256]{1,0:T(8,128)(2,1)}) fusion(bf16[2,256,256]{2,1,0:T(8,128)(2,1)} %block.1), kind=kLoop, calls=%fused_computation | loop fusion | bytes 524288 | tf_op jit(solution)/shard_map/squeeze | solution.py:738

commit v8 on v7

--- a/solution.py
+++ b/solution.py
@@ -387,7 +387,7 @@
     hid_s, cot_s, wq_s, wo_s, wkv_s, wkv_w, wkv_f, kv_s,
     q_s, d_s, q_land, last, a_s, a_land,
     part_o, sib_o, acc_o, land_o, part_g, sib_g, acc_g, zland_g, land_g,
-    part_t, sib_t, acc_t, land_t, sum_o, prob_s,
+    part_t, sib_t, acc_t, zland_t, land_t, sum_o, prob_s,
     wq, wo, wkv, tab_sem, send_sem, recv_sem,
 ):
     p = Place()
@@ -645,8 +645,8 @@
     def keep_head(rows, total):
         sum_o[rows, :] = total
 
-    def keep_tail(total):
-        sum_o[tail, :] = total
+    def keep_tail(rows, total):
+        sum_o[pl.ds(192 + rows.start, rows.size), :] = total
 
     blocks = pl.ds(0, 15)
     body_rows, every = pl.ds(0, 192), slice(None)
@@ -657,9 +657,9 @@
         w, p, w.group(wq_s.at[blocks, body_rows]),
         part_g, sib_g, acc_g, zland_g, land_g, keep_head,
     )
-    rt = scatter_mp(
+    rt = scatter_zy(
         w, p, w.group(wq_s.at[blocks, pl.ds(0, 64)]),
-        part_t, sib_t, acc_t, land_t, keep_tail, False,
+        part_t, sib_t, acc_t, zland_t, land_t, keep_tail,
     )
     attend((0, 1, 2))
     differentiate((0, 1, 2))
@@ -676,7 +676,6 @@
     next(ro)
     fill(0, wo_s, part_o, p.c, every)
     next(ro)
-    next(rg)
     take_back(1, *back_g)
     fill(1, wq_s, part_t, 1 - p.c, tail)
     next(rt)
@@ -684,13 +683,15 @@
     next(rt)
     next(rg)
     next(ro)
+    next(rg)
     next(rt)
+    next(rt)
+    next(ro)
     next(rg)
-    next(ro)
     next(rt)
     next(rg, None)
+    next(rt, None)
     next(ro, None)
-    next(rt, None)
     res[1] = pltpu.roll(sum_o[...], 63, 0).astype(BF16)
     w.finish()
 
@@ -703,7 +704,7 @@
     row = (64, 896)
     bf = lambda *s: pltpu.VMEM(s, BF16)
     vm = pl.BlockSpec(memory_space=pltpu.VMEM)
-    messages, groups = 132, 18
+    messages, groups = 135, 18
     res = pl.pallas_call(
         body,
         out_shape=jax.ShapeDtypeStruct((2,) + blk, BF16),
@@ -721,7 +722,7 @@
             bf(*blk), bf(*blk), bf(2, 64, 256), bf(2, 64, 256), bf(2, *blk), bf(2, 64, 256),
             bf(8, 2, *blk), bf(8, *blk), bf(8, *blk), bf(7, *blk),
             bf(8, 2, 192, 256), bf(8, 192, 256), bf(8, 192, 256), bf(4, 192, 256), bf(6, 96, 256),
-            bf(8, 2, 64, 256), bf(8, 64, 256), bf(8, 64, 256), bf(7, 64, 256),
+            bf(8, 2, 64, 256), bf(8, 64, 256), bf(8, 64, 256), bf(4, 64, 256), bf(6, 32, 256),
             pltpu.VMEM(blk, F32), pltpu.VMEM((8, 64, 256), F32),
             bf(*blk), bf(*blk), bf(56, 512),
             pltpu.SemaphoreType.DMA,

time: 101 us -> 100 us (0.990)
  Pallas kernels: 98.9 us -> 97.5 us
    pallas_call x1, Pallas kernels: 98.9 us -> 97.5 us  [per_device(): pl.pallas_call(body, out_shape=jax.ShapeDtypeStruct((2,) + blk, BF16), in...]
where the time goes in v8:
time: 100 us; the launch traced here: 99.8 us
  Pallas kernels  97.5 us (98%)
  local copies, waits for them, and re-layouts  1.68 us (2%)
    pallas_call x1, Pallas kernels, per_device(): pl.pallas_call(body, out_shape=jax.ShapeDtypeStruct((2,) + blk, BF16), in...  97.5 us

profile of v8, /device:TPU:1, one launch (start us, length us, event | category | flops | bytes accessed | tf_op | source)
XLA Modules:
  0.0 99.8 jit_solution(5550585667448783678)
XLA Ops:
  0.6 97.5 %block.1 = bf16[2,256,256]{2,1,0:T(8,128)(2,1)} custom-call(bf16[256,256]{1,0:T(8,128)(2,1)} %hid.1, bf16[256,256]{1,0:T(8,128)(2,1)} %cot.1, bf16[256,2,128]{2,1,0:T(2,128)(2,1)} %wq3.1, bf16[256,2,128]{2,1,0:T(2,128)(2,1)} %wo3.1, bf16[56,2,2,128]{3,2,1,0:T(2,128)(2,1)} %wkv3.1, bf16[4000,896]{1,0:T(8,128)(2,1)} %table.1, s32[8,128]{1,0:T(8,128)} %bitcast.6, ...), custom_call_target="tpu_custom_call" | custom-call | tf_op jit(solution)/shard_map/block/pallas_call | solution.py:708
  98.2 1.7 %slice_bitcast_fusion = (bf16[256,256]{1,0:T(8,128)(2,1)}, bf16[256,256]{1,0:T(8,128)(2,1)}) fusion(bf16[2,256,256]{2,1,0:T(8,128)(2,1)} %block.1), kind=kLoop, calls=%fused_computation | loop fusion | bytes 524288 | tf_op jit(solution)/shard_map/squeeze | solution.py:739
